TPU v7x, 32 devices: a whole 2x2x4 slice. The times are simulated.
32 devices in a mesh: shard: 8 (over y, x, core), rep: 4 (over z).
Axes of the slice: x: 2, y: 2, z: 4, core: 2. Of those that a mesh axis runs over, the one named last changes fastest.
Arguments:
- tokens: bfloat16 [2, 16384, 768], P(None, ('shard', 'rep')), may hold values from -6 to 6
- segment_ids: int32 [2, 16384], P(None, ('shard', 'rep')), may hold values from 0 to 7, as said below
- qkv_weight: bfloat16 [768, 2304], P('shard'), may hold values from -0.21875 to 0.21875
- out_weight: bfloat16 [768, 768], P('shard'), may hold values from -0.875 to 0.875
- gate_weight: bfloat16 [768, 3072], P('shard'), may hold values from -0.21875 to 0.21875
- up_weight: bfloat16 [768, 3072], P('shard'), may hold values from -0.21875 to 0.21875
- down_weight: bfloat16 [3072, 768], P('shard'), may hold values from -0.109375 to 0.109375
- norm1_gain: bfloat16 [768], P('shard'), may hold values from 0.5 to 1.5
- norm1_bias: bfloat16 [768], P('shard'), may hold values from -1 to 1
- norm2_gain: bfloat16 [768], P('shard'), may hold values from 0.5 to 1.5
- norm2_bias: bfloat16 [768], P('shard'), may hold values from -1 to 1
- out_grad: bfloat16 [2, 16384, 768], P(None, ('shard', 'rep')), may hold values from -6 to 6
Outputs:
- output: bfloat16 [2, 16384, 768], P(None, ('shard', 'rep'))
- input_grad: bfloat16 [2, 16384, 768], P(None, ('shard', 'rep'))
- qkv_weight_grad: float32 [768, 2304], P('shard')
- out_weight_grad: float32 [768, 768], P('shard')
- gate_weight_grad: float32 [768, 3072], P('shard')
- up_weight_grad: float32 [768, 3072], P('shard')
- down_weight_grad: float32 [3072, 768], P('shard')
- norm1_gain_grad: float32 [768], P('shard')
- norm1_bias_grad: float32 [768], P('shard')
- norm2_gain_grad: float32 [768], P('shard')
- norm2_bias_grad: float32 [768], P('shard')
Inputs may be any that keep to these rules, and one draw needn't show every extreme that they name: Within each packed sequence of 512 tokens segment_ids never falls, starts at 0, and takes each value 0 to 7 on a run of one or more tokens.
All inputs are finite; a program needn't handle non-finite values.
Results may differ from a plain program's by a relative error of at most 0.02.
Values may be sent and summed in bfloat16 or wider, within the bound.
No kernel may reach another device: no remote copies, remote signals or barrier semaphores. Data moves between devices by JAX's collectives and lax.ppermute only.
A program may use at most 192 MiB of HBM per device.

v0:
```python
import jax
import jax.numpy as jnp
from jax import lax
from jax.sharding import PartitionSpec as P

HEAD_DIM = 64


norm_eps = 1e-12
rope_base = 1000.0
masked_score = -1000000000.0


def matmul(left_op, right_op):
    return jnp.dot(left_op, right_op, preferred_element_type=jnp.float32)


def inner_sum(left_op, right_op):
    return lax.dot_general(
        left_op, right_op, (((0,), (0,)), ((), ())), preferred_element_type=jnp.float32
    )


def times_transposed(left_op, right_op):
    return lax.dot_general(
        left_op, right_op, (((1,), (1,)), ((), ())), preferred_element_type=jnp.float32
    )


def rope_tables(seq_len, head_dim):
    places = jnp.arange(seq_len, dtype=jnp.int32).astype(jnp.float32)
    frequency = rope_base ** (-jnp.arange(0, head_dim, 2, dtype=jnp.float32) / head_dim)
    angles = places[:, None] * frequency[None, :]
    cos_table = jnp.cos(angles)
    sin_table = jnp.sin(angles)
    return (
        jnp.concatenate([cos_table, cos_table], -1),
        jnp.concatenate([sin_table, sin_table], -1),
    )


def rotate(values, cos_table, sin_table):
    half_dim = values.shape[-1] // 2
    turned = jnp.concatenate([-values[..., half_dim:], values[..., :half_dim]], -1)
    return values * cos_table + turned * sin_table


def rotate_back(grad_in, cos_table, sin_table):
    half_dim = grad_in.shape[-1] // 2
    scaled = grad_in * sin_table
    turned = jnp.concatenate([scaled[..., half_dim:], -scaled[..., :half_dim]], -1)
    return grad_in * cos_table + turned


def normalize(hidden_in):
    centre = hidden_in - jnp.mean(hidden_in, -1, keepdims=True)
    inv_std = lax.rsqrt(jnp.mean(centre * centre, -1, keepdims=True) + norm_eps)
    return (centre * inv_std, inv_std)


def norm_back(grad_norm, normed, inv_std):
    return inv_std * (
        grad_norm
        - jnp.mean(grad_norm, -1, keepdims=True)
        - normed * jnp.mean(grad_norm * normed, -1, keepdims=True)
    )


def attend_head(query_h, key_h, value_h, same_doc):
    scores = jnp.where(same_doc, times_transposed(query_h, key_h) * 0.125, masked_score)
    row_max = jnp.max(scores, -1, keepdims=True)
    expo = jnp.exp(scores - row_max)
    total_sum = jnp.sum(expo, -1, keepdims=True)
    probs = expo / total_sum
    result = matmul(probs.astype(jnp.bfloat16), value_h)
    return (result, (row_max + jnp.log(total_sum))[:, 0])


def head_backward(query_h, key_h, value_h, grad_h, log_total, same_doc):
    scores = jnp.where(same_doc, times_transposed(query_h, key_h) * 0.125, masked_score)
    probs = jnp.exp(scores - log_total[:, None])
    grad_value = inner_sum(probs.astype(jnp.bfloat16), grad_h)
    grad_probs = times_transposed(grad_h, value_h)
    grad_scores = (probs * (grad_probs - jnp.sum(probs * grad_probs, -1, keepdims=True))).astype(
        jnp.bfloat16
    )
    grad_query = matmul(grad_scores, key_h) * 0.125
    grad_key = inner_sum(grad_scores, query_h) * 0.125
    return (grad_query, grad_key, grad_value)


def forward_pass(token_rows, segment, weight_set):
    full_qkv, full_out, full_gate, full_up, full_down, gain_one, bias_one, gain_two, bias_two = (
        weight_set
    )
    seq_len = token_rows.shape[0]
    width = full_out.shape[0]
    head_count = width // HEAD_DIM
    cos_table, sin_table = rope_tables(seq_len, HEAD_DIM)
    cos_heads = cos_table[:, None, :]
    sin_heads = sin_table[:, None, :]
    joint = matmul(token_rows, full_qkv)
    queries = (
        rotate(joint[:, :width].reshape(seq_len, head_count, HEAD_DIM), cos_heads, sin_heads)
        .astype(jnp.bfloat16)
        .transpose(1, 0, 2)
    )
    key_rows = (
        rotate(
            joint[:, width : 2 * width].reshape(seq_len, head_count, HEAD_DIM), cos_heads, sin_heads
        )
        .astype(jnp.bfloat16)
        .transpose(1, 0, 2)
    )
    value_rows = (
        joint[:, 2 * width :]
        .reshape(seq_len, head_count, HEAD_DIM)
        .astype(jnp.bfloat16)
        .transpose(1, 0, 2)
    )
    same_doc = segment[:, None] == segment[None, :]
    attended, log_total = lax.map(
        lambda operands: attend_head(operands[0], operands[1], operands[2], same_doc),
        (queries, key_rows, value_rows),
    )
    attended_low = attended.transpose(1, 0, 2).reshape(seq_len, width).astype(jnp.bfloat16)
    residual_one = token_rows.astype(jnp.float32) + matmul(attended_low, full_out)
    normed_one, inv_one = normalize(residual_one)
    mixed = normed_one * gain_one.astype(jnp.float32) + bias_one.astype(jnp.float32)
    mixed_low = mixed.astype(jnp.bfloat16)
    gate_pre = matmul(mixed_low, full_gate)
    up_pre = matmul(mixed_low, full_up)
    sigmoid_gate = jax.nn.sigmoid(gate_pre)
    hidden_low = (gate_pre * sigmoid_gate * up_pre).astype(jnp.bfloat16)
    residual_two = mixed + matmul(hidden_low, full_down)
    normed_two, inv_two = normalize(residual_two)
    layer_out = (normed_two * gain_two.astype(jnp.float32) + bias_two.astype(jnp.float32)).astype(
        jnp.bfloat16
    )
    kept = {
        "token_rows": token_rows,
        "cos_heads": cos_heads,
        "sin_heads": sin_heads,
        "queries": queries,
        "key_rows": key_rows,
        "value_rows": value_rows,
        "log_total": log_total,
        "same_doc": same_doc,
        "attended_low": attended_low,
        "normed_one": normed_one,
        "inv_one": inv_one,
        "mixed_low": mixed_low,
        "gate_pre": gate_pre,
        "up_pre": up_pre,
        "sigmoid_gate": sigmoid_gate,
        "hidden_low": hidden_low,
        "normed_two": normed_two,
        "inv_two": inv_two,
    }
    return (kept, layer_out)


def backward_pass(kept, weight_set, cotangent):
    full_qkv, full_out, full_gate, full_up, full_down, gain_one, gain_two = weight_set
    token_rows = kept["token_rows"]
    seq_len = token_rows.shape[0]
    width = full_out.shape[0]
    head_count = width // HEAD_DIM
    grad_gain_two = jnp.sum(cotangent * kept["normed_two"], 0)
    grad_bias_two = jnp.sum(cotangent, 0)
    grad_res_two = norm_back(
        cotangent * gain_two.astype(jnp.float32), kept["normed_two"], kept["inv_two"]
    )
    grad_mlp = grad_res_two.astype(jnp.bfloat16)
    grad_down = inner_sum(kept["hidden_low"], grad_mlp)
    grad_hidden = times_transposed(grad_mlp, full_down)
    gate_pre = kept["gate_pre"]
    sigmoid_gate = kept["sigmoid_gate"]
    grad_up_pre = (grad_hidden * gate_pre * sigmoid_gate).astype(jnp.bfloat16)
    grad_gate_pre = (
        grad_hidden * kept["up_pre"] * sigmoid_gate * (1.0 + gate_pre * (1.0 - sigmoid_gate))
    ).astype(jnp.bfloat16)
    grad_gate = inner_sum(kept["mixed_low"], grad_gate_pre)
    grad_up = inner_sum(kept["mixed_low"], grad_up_pre)
    grad_mixed = (
        grad_res_two
        + times_transposed(grad_gate_pre, full_gate)
        + times_transposed(grad_up_pre, full_up)
    )
    grad_gain_one = jnp.sum(grad_mixed * kept["normed_one"], 0)
    grad_bias_one = jnp.sum(grad_mixed, 0)
    grad_res_one = norm_back(
        grad_mixed * gain_one.astype(jnp.float32), kept["normed_one"], kept["inv_one"]
    )
    grad_branch = grad_res_one.astype(jnp.bfloat16)
    grad_out = inner_sum(kept["attended_low"], grad_branch)
    grad_att = (
        times_transposed(grad_branch, full_out)
        .astype(jnp.bfloat16)
        .reshape(seq_len, head_count, HEAD_DIM)
        .transpose(1, 0, 2)
    )
    same_doc = kept["same_doc"]
    grad_query, grad_key, grad_value = lax.map(
        lambda operands: head_backward(
            operands[0], operands[1], operands[2], operands[3], operands[4], same_doc
        ),
        (kept["queries"], kept["key_rows"], kept["value_rows"], grad_att, kept["log_total"]),
    )
    query_part = rotate_back(
        grad_query.transpose(1, 0, 2), kept["cos_heads"], kept["sin_heads"]
    ).reshape(seq_len, width)
    key_part = rotate_back(
        grad_key.transpose(1, 0, 2), kept["cos_heads"], kept["sin_heads"]
    ).reshape(seq_len, width)
    value_part = grad_value.transpose(1, 0, 2).reshape(seq_len, width)
    grad_joint = jnp.concatenate([query_part, key_part, value_part], -1).astype(jnp.bfloat16)
    grad_qkv = inner_sum(token_rows, grad_joint)
    input_grad = (grad_res_one + times_transposed(grad_joint, full_qkv)).astype(jnp.bfloat16)
    return (
        (
            grad_qkv,
            grad_out,
            grad_gate,
            grad_up,
            grad_down,
            grad_gain_one,
            grad_bias_one,
            grad_gain_two,
            grad_bias_two,
        ),
        input_grad,
    )


def shards(
    tokens,
    segment_ids,
    qkv_weight,
    out_weight,
    gate_weight,
    up_weight,
    down_weight,
    norm1_gain,
    norm1_bias,
    norm2_gain,
    norm2_bias,
    out_grad,
):
    owned_shards = (
        qkv_weight,
        out_weight,
        gate_weight,
        up_weight,
        down_weight,
        norm1_gain,
        norm1_bias,
        norm2_gain,
        norm2_bias,
    )
    group_count = lax.axis_size("shard")
    summed = tuple(
        (
            jnp.zeros((weight_piece.shape[0] * group_count,) + weight_piece.shape[1:], jnp.float32)
            for weight_piece in owned_shards
        )
    )
    outputs = []
    input_grads = []
    for micro_step in range(tokens.shape[0]):
        forward_set = (
            lax.all_gather(qkv_weight, "shard", axis=0, tiled=True),
            lax.all_gather(out_weight, "shard", axis=0, tiled=True),
            lax.all_gather(gate_weight, "shard", axis=0, tiled=True),
            lax.all_gather(up_weight, "shard", axis=0, tiled=True),
            lax.all_gather(down_weight, "shard", axis=0, tiled=True),
            lax.all_gather(norm1_gain, "shard", axis=0, tiled=True),
            lax.all_gather(norm1_bias, "shard", axis=0, tiled=True),
            lax.all_gather(norm2_gain, "shard", axis=0, tiled=True),
            lax.all_gather(norm2_bias, "shard", axis=0, tiled=True),
        )
        kept, layer_out = forward_pass(tokens[micro_step], segment_ids[micro_step], forward_set)
        backward_set = (
            lax.all_gather(qkv_weight, "shard", axis=0, tiled=True),
            lax.all_gather(out_weight, "shard", axis=0, tiled=True),
            lax.all_gather(gate_weight, "shard", axis=0, tiled=True),
            lax.all_gather(up_weight, "shard", axis=0, tiled=True),
            lax.all_gather(down_weight, "shard", axis=0, tiled=True),
            lax.all_gather(norm1_gain, "shard", axis=0, tiled=True),
            lax.all_gather(norm2_gain, "shard", axis=0, tiled=True),
        )
        grad_set, input_grad = backward_pass(
            kept, backward_set, out_grad[micro_step].astype(jnp.float32)
        )
        outputs.append(layer_out)
        input_grads.append(input_grad)
        summed = tuple((left_sum + right_sum for left_sum, right_sum in zip(summed, grad_set)))
    (
        sum_qkv,
        sum_out,
        sum_gate,
        sum_up,
        sum_down,
        sum_gain_one,
        sum_bias_one,
        sum_gain_two,
        sum_bias_two,
    ) = summed
    summed = (
        lax.psum_scatter(
            sum_qkv.astype(jnp.bfloat16), "shard", scatter_dimension=0, tiled=True
        ).astype(jnp.float32),
        lax.psum_scatter(
            sum_out.astype(jnp.bfloat16), "shard", scatter_dimension=0, tiled=True
        ).astype(jnp.float32),
        lax.psum_scatter(
            sum_gate.astype(jnp.bfloat16), "shard", scatter_dimension=0, tiled=True
        ).astype(jnp.float32),
        lax.psum_scatter(
            sum_up.astype(jnp.bfloat16), "shard", scatter_dimension=0, tiled=True
        ).astype(jnp.float32),
        lax.psum_scatter(
            sum_down.astype(jnp.bfloat16), "shard", scatter_dimension=0, tiled=True
        ).astype(jnp.float32),
        lax.psum_scatter(
            sum_gain_one.astype(jnp.bfloat16), "shard", scatter_dimension=0, tiled=True
        ).astype(jnp.float32),
        lax.psum_scatter(
            sum_bias_one.astype(jnp.bfloat16), "shard", scatter_dimension=0, tiled=True
        ).astype(jnp.float32),
        lax.psum_scatter(
            sum_gain_two.astype(jnp.bfloat16), "shard", scatter_dimension=0, tiled=True
        ).astype(jnp.float32),
        lax.psum_scatter(
            sum_bias_two.astype(jnp.bfloat16), "shard", scatter_dimension=0, tiled=True
        ).astype(jnp.float32),
    )
    (
        part_qkv,
        part_out,
        part_gate,
        part_up,
        part_down,
        part_gain_one,
        part_bias_one,
        part_gain_two,
        part_bias_two,
    ) = summed
    totals = (
        lax.psum(part_qkv.astype(jnp.bfloat16), "rep").astype(jnp.float32),
        lax.psum(part_out.astype(jnp.bfloat16), "rep").astype(jnp.float32),
        lax.psum(part_gate.astype(jnp.bfloat16), "rep").astype(jnp.float32),
        lax.psum(part_up.astype(jnp.bfloat16), "rep").astype(jnp.float32),
        lax.psum(part_down.astype(jnp.bfloat16), "rep").astype(jnp.float32),
        lax.psum(part_gain_one.astype(jnp.bfloat16), "rep").astype(jnp.float32),
        lax.psum(part_bias_one.astype(jnp.bfloat16), "rep").astype(jnp.float32),
        lax.psum(part_gain_two.astype(jnp.bfloat16), "rep").astype(jnp.float32),
        lax.psum(part_bias_two.astype(jnp.bfloat16), "rep").astype(jnp.float32),
    )
    return (
        jnp.stack(outputs),
        jnp.stack(input_grads),
        totals[0],
        totals[1],
        totals[2],
        totals[3],
        totals[4],
        totals[5],
        totals[6],
        totals[7],
        totals[8],
    )


def solution(mesh):
    in_specs = (
        P(None, ("shard", "rep"), None),
        P(None, ("shard", "rep")),
        P("shard", None),
        P("shard", None),
        P("shard", None),
        P("shard", None),
        P("shard", None),
        P("shard"),
        P("shard"),
        P("shard"),
        P("shard"),
        P(None, ("shard", "rep"), None),
    )
    out_specs = (
        P(None, ("shard", "rep"), None),
        P(None, ("shard", "rep"), None),
        P("shard", None),
        P("shard", None),
        P("shard", None),
        P("shard", None),
        P("shard", None),
        P("shard"),
        P("shard"),
        P("shard"),
        P("shard"),
    )
    return jax.shard_map(shards, mesh=mesh, in_specs=in_specs, out_specs=out_specs, check_vma=False)
```

profile of v0, /device:TPU:0, one launch (start us, length us, event | category | flops | bytes accessed | tf_op | source)
XLA Modules:
  0.0 871.9 jit_solution(1877780145343959413)
XLA Ops:
  14.7 15.5 %all-reduce.9 = (bf16[768]{0:T(1024)(128)(2,1)S(1)}, bf16[768]{0:T(1024)(128)(2,1)S(1)}, bf16[768]{0:T(1024)(128)(2,1)S(1)}) all-reduce(bf16[768]{0:T(1024)(128)(2,1)S(1)} %dynamic-update-slice.1, bf16[768]{0:T(1024)(128)(2,1)S(1)} %dynamic-update-slice, ...), channel_id=1, replica_groups=mesh['shard'=8,'rep'=4] {'shard'}, use_global_device_ids=true, to_apply=%add.1 | all-reduce | flops 2304 | bytes 9216
  30.6 16.1 %all-gather.6.cloned.1.call-done = bf16[768,2304]{1,0:T(8,128)(2,1)} async-done(((bf16[96,2304]{1,0:T(8,128)(2,1)}), bf16[768,2304]{1,0:T(8,128)(2,1)}) %all-gather.6.cloned.1.call-update) | async-done | bytes 3538960 | tf_op jit(solution)/shard_map/all_gather | solution.py:272
  46.8 4.3 fusion.135
  54.6 2.0 fusion.138
  56.6 1.9 fusion.166
  59.9 1.9 copy.72
  61.8 3.0 copy.65
  64.8 3.2 copy.66
  70.5 2.8 fusion.132
  78.6 33.0 %while.57 = (s32[]{:T(128)}, bf16[12,512,64]{1,2,0:T(8,128)(2,1)S(1)}, f32[12,512]{1,0:T(8,128)S(1)}, bf16[12,512,64]{2,1,0:T(8,128)(2,1)S(1)}, bf16[12,512,64]{...) while((s32[]{:T(128)}, ...), condition=%wide.region_11.12_spmd.clone, body=%wide.region_8.11_spmd.clone.sunk | while | flops 69467648 | bytes 3696737 | solution.py:122
  111.7 3.0 copy.68
  119.1 34.0 %while.56 = (s32[]{:T(128)}, bf16[12,512,64]{1,2,0:T(8,128)(2,1)S(1)}, f32[12,512]{1,0:T(8,128)S(1)}, bf16[12,512,64]{2,1,0:T(8,128)(2,1)}, bf16[12,512,64]{2,1,...) while((s32[]{:T(128)}, ...), condition=%wide.region_3.4_spmd.clone, body=%wide.region_0.3_spmd.clone.sunk | while | flops 69467648 | bytes 3696737 | solution.py:122
  153.2 2.7 fusion.176
  161.3 7.5 fusion.180
  168.8 9.0 %multiply_convert_fusion.6 = (bf16[512,3072]{1,0:T(8,128)(2,1)}, f32[512,3072]{1,0:T(8,128)}) fusion(f32[512,3072]{1,0:T(8,128)} %fusion.180, bf16[512,768]{1,0:T(8,128)(2,1)S(1)} %get-tuple-element.540, bf16[768,3072]{1,0:T(8,128)(2,1)} %all-gather.12.cloned.1.call-done), kind=kOutput, calls=%fused_computation.120 | convolution fusion | flops 2425356288 | bytes 21233664 | tf_op jit(solution)/shard_map/dot_general | solution.py:15
  177.8 17.1 %all-gather.14.cloned.1.call-done = bf16[3072,768]{1,0:T(8,128)(2,1)} async-done(((bf16[384,768]{1,0:T(8,128)(2,1)}), bf16[3072,768]{1,0:T(8,128)(2,1)}) %all-gather.14.cloned.1.call-update) | async-done | bytes 4718608 | tf_op jit(solution)/shard_map/all_gather | solution.py:276
  195.0 6.1 fusion.178
  202.3 2.6 fusion.179
  204.9 5.1 multiply_convert_fusion.7
  210.0 2.8 fusion.177
  214.8 2.2 fusion.106
  217.0 9.5 %multiply_convert_fusion.4 = (bf16[512,3072]{1,0:T(8,128)(2,1)}, bf16[512,3072]{1,0:T(8,128)(2,1)}) fusion(f32[512,3072]{1,0:T(8,128)S(1)} %fusion.179, f32[512,3072]{1,0:T(8,128)} %get-tuple-element.553, bf16[3072,768]{1,0:T(8,128)(2,1)} %all-gather.14.cloned.1.call-done, f32[512]{0:T(512)S(1)} %broadcast_multiply_fusion.6, ...), kind=kOutput, calls=%fused_computation.118 | convolution fusion | flops 2439905280 | bytes 25964544 | tf_op jit(solution)/shard_map/dot_general | solution.py:25
  226.5 4.8 fusion.181
  231.3 7.1 multiply_reduce_fusion.3
  238.5 10.0 %multiply_convert_fusion.2 = (bf16[512,3072]{1,0:T(8,128)(2,1)}, bf16[512,3072]{1,0:T(8,128)(2,1)}) fusion(f32[512,3072]{1,0:T(8,128)S(1)} %bitcast.388, f32[512,3072]{1,0:T(8,128)} %get-tuple-element.557, bf16[3072,768]{1,0:T(8,128)(2,1)} %all-gather.14.cloned.1.call-done, f32[512]{0:T(512)S(1)} %broadcast_multiply_fusion.2, ...), kind=kOutput, calls=%fused_computation.116 | convolution fusion | flops 2439905280 | bytes 25964544 | tf_op jit(solution)/shard_map/dot_general | solution.py:25
  248.5 4.8 fusion.182
  253.3 7.2 multiply_reduce_fusion.2
  263.5 2.3 copy.77
  268.5 99.7 %while.58 = (s32[]{:T(128)}, f32[12,512,64]{1,2,0:T(8,128)}, f32[12,512,64]{1,2,0:T(8,128)}, bf16[12,512,64]{1,2,0:T(8,128)(2,1)}, bf16[12,512,64]{2,1,0:T(8,128...) while((s32[]{:T(128)}, f32[12,512,64]{1,2,0:T(8,128)}, ...), condition=%wide.region_22.23_spmd.clone, body=%wide.region_20.22_spmd.clone.sunk | while | flops 170458624 | bytes 9063537 | solution.py:204
  271.4 1.9 fusion.283
  296.3 1.9 fusion.283
  368.2 1.9 subtract_multiply_fusion
  374.8 92.1 %while.59 = (s32[]{:T(128)}, f32[12,512,64]{1,2,0:T(8,128)S(1)}, f32[12,512,64]{1,2,0:T(8,128)}, bf16[12,512,64]{1,2,0:T(8,128)(2,1)}, bf16[12,512,64]{2,1,0:T(8...) while((s32[]{:T(128)}, f32[12,512,64]{1,2,0:T(8,128)S(1)}, ...), condition=%wide.region_29.30_spmd.clone, body=%wide.region_27.29_spmd.clone.sunk | while | flops 170458624 | bytes 9063537 | solution.py:204
  377.9 1.9 fusion.295
  385.5 1.9 fusion.295
  400.8 1.9 fusion.295
  408.5 1.9 fusion.295
  423.8 1.9 fusion.295
  446.8 1.9 fusion.295
  462.1 1.9 fusion.295
  466.9 3.1 multiply_bitcast_fusion.3
  472.9 2.9 fusion.119
  475.7 4.5 fusion.127
  480.3 5.1 fusion.92
  485.4 5.8 copy.88
  492.4 2.3 fusion.149
  496.8 6.0 fusion.152
  502.9 5.4 add_convert_fusion
  509.4 4.7 fusion.184
  514.2 4.6 add_convert_fusion.1
  519.2 4.7 fusion.183
  523.9 4.6 add_convert_fusion.2
  530.3 9.2 %reduce-scatter.16.cloned.1.call-done = bf16[96,2304]{1,0:T(8,128)(2,1)} async-done(((bf16[768,2304]{1,0:T(8,128)(2,1)}), bf16[96,2304]{1,0:T(8,128)(2,1)}) %reduce-scatter.16.cloned.1.call-update) | async-done | bytes 442384
  539.5 2.1 copy.89
  541.6 38.5 %reduce-scatter.8.cloned.1.call-done = bf16[96,768]{1,0:T(8,128)(2,1)} async-done(((bf16[768,768]{1,0:T(8,128)(2,1)}), bf16[96,768]{1,0:T(8,128)(2,1)}) %reduce-scatter.8.cloned.1.call-update) | async-done | bytes 147472 | tf_op jit(solution)/shard_map/reduce_scatter | solution.py:313
  580.1 57.8 %reduce-scatter.14.cloned.1.call-done = bf16[384,768]{1,0:T(8,128)(2,1)} async-done(((bf16[3072,768]{1,0:T(8,128)(2,1)}), bf16[384,768]{1,0:T(8,128)(2,1)}) %reduce-scatter.14.cloned.1.call-update) | async-done | bytes 589840 | tf_op jit(solution)/shard_map/reduce_scatter | solution.py:322
  637.9 57.4 %reduce-scatter.12.cloned.1.call-done = bf16[96,3072]{1,0:T(8,128)(2,1)} async-done(((bf16[768,3072]{1,0:T(8,128)(2,1)}), bf16[96,3072]{1,0:T(8,128)(2,1)}) %reduce-scatter.12.cloned.1.call-update) | async-done | bytes 589840 | tf_op jit(solution)/shard_map/reduce_scatter | solution.py:319
  695.3 57.6 %reduce-scatter.10.cloned.1.call-done = bf16[96,3072]{1,0:T(8,128)(2,1)} async-done(((bf16[768,3072]{1,0:T(8,128)(2,1)}), bf16[96,3072]{1,0:T(8,128)(2,1)}) %reduce-scatter.10.cloned.1.call-update) | async-done | bytes 589840 | tf_op jit(solution)/shard_map/reduce_scatter | solution.py:316
  753.0 23.9 %all-reduce.8 = (bf16[768]{0:T(1024)(128)(2,1)S(1)}, bf16[768]{0:T(1024)(128)(2,1)S(1)}, bf16[768]{0:T(1024)(128)(2,1)S(1)}, bf16[768]{0:T(1024)(128)(2,1)S(1)}, bf16[768]{0:T(1024)(128)(2,1)S(1)}) all-reduce(bf16[768]{0:T(1024)(128)(2,1)S(1)} %dynamic-update-slice.3, ...), channel_id=1, replica_groups=mesh['shard'=8,'rep'=4] {'shard'}, use_global_device_ids=true, to_apply=%add.3 | all-reduce | flops 3840 | bytes 15360
  777.1 12.4 %all-reduce.10 = (bf16[96]{0:T(256)(128)(2,1)S(1)}, bf16[96]{0:T(256)(128)(2,1)S(1)}, bf16[96]{0:T(256)(128)(2,1)S(1)}, bf16[96]{0:T(256)(128)(2,1)S(1)}) all-reduce(bf16[96]{0:T(256)(128)(2,1)S(1)} %dynamic-slice.5, bf16[96]{0:T(256)(128)(2,1)S(1)} %dynamic-slice.7, ...), channel_id=1, replica_groups=mesh['shard'=8,'rep'=4] {'rep'}, use_global_device_ids=true, to_apply=%region_43.44 | all-reduce | flops 384 | bytes 1536 | tf_op jit(solution)/shard_map/psum | solution.py:355
  791.6 4.9 fusion.125
  796.6 3.2 fusion.126
  803.6 54.9 %all-reduce.14.cloned.1.call-done = (bf16[96,2304]{0,1:T(8,128)(2,1)}, bf16[96,768]{1,0:T(8,128)(2,1)}, bf16[96,3072]{1,0:T(8,128)(2,1)}, bf16[96,3072]{1,0:T(8,128)(2,1)}, bf16[384,768]{1,0:T(8,128)(2,1)}) async-done(((bf16[96,2304]{0,1:T(8,128)(2,1)}, bf16[96,768]{1,0:T(8,128)(2,1)}, bf16[96,3072]{1,0:T(8,128)(2,1)}, bf16[96,3072]{1,0:T(8,128)(2,1)}, bf16[384,768]{1,0:T(8,128)(2,1)}), ...) | async-done | bytes 2359312 | tf_op jit(solution)/shard_map/psum | solution.py:350
  858.5 2.3 convert_element_type.286
  (558 shorter events, 302.2 us)
Async XLA Ops:
  7.2 39.6 %all-gather.6.cloned.1.call-start = ((), (), s32[]{:S(2)}) async-start(), calls=%async_computation.5 | async-start | bytes 3981312 | tf_op jit(solution)/shard_map/all_gather | solution.py:272
  7.9 145.3 %all-gather.8.cloned.1.call-start = ((), (), s32[]{:S(2)}) async-start(), calls=%async_computation.6 | async-start | bytes 1327104 | tf_op jit(solution)/shard_map/all_gather | solution.py:273
  8.7 152.7 %all-gather.10.cloned.1.call-start = ((), (), s32[]{:S(2)}) async-start(), calls=%async_computation.7 | async-start | bytes 5308416 | tf_op jit(solution)/shard_map/all_gather | solution.py:274
  9.4 159.4 %all-gather.12.cloned.1.call-start = ((), (), s32[]{:S(2)}) async-start(), calls=%async_computation.8 | async-start | bytes 5308416 | tf_op jit(solution)/shard_map/all_gather | solution.py:275
  10.0 185.0 %all-gather.14.cloned.1.call-start = ((), (), s32[]{:S(2)}) async-start(), calls=%async_computation.9 | async-start | bytes 5308416 | tf_op jit(solution)/shard_map/all_gather | solution.py:276
  10.6 528.9 %reduce-scatter.16.cloned.1.call-start = ((), (), s32[]{:S(2)}) async-start(), calls=%async_computation.14 | async-start | bytes 3981312
  10.8 3.2 copy-start.62
  10.8 3.5 copy-start.63
  10.8 3.7 copy-start.64
  30.6 39.9 %copy-start.38 = (f32[512,64]{0,1:T(8,128)}, f32[512,64]{0,1:T(8,128)S(1)}, u32[]{:S(2)}) copy-start(f32[512,64]{0,1:T(8,128)S(1)} %get-tuple-element.562) | copy-start | bytes 393220
  30.6 39.9 %copy-start.40 = (f32[512,64]{0,1:T(8,128)}, f32[512,64]{0,1:T(8,128)S(1)}, u32[]{:S(2)}) copy-start(f32[512,64]{0,1:T(8,128)S(1)} %get-tuple-element.563) | copy-start | bytes 393220
  51.0 2.9 copy-start.54
  111.6 4.5 copy-start.4
  111.7 4.5 copy-start.29
  111.7 3.0 copy-start.30
  119.1 34.0 %copy-start.5 = (bf16[12,512,64]{1,2,0:T(8,128)(2,1)S(1)}, bf16[12,512,64]{1,2,0:T(8,128)(2,1)}, u32[]{:S(2)}) copy-start(bf16[12,512,64]{1,2,0:T(8,128)(2,1)} %copy-done.4) | copy-start | bytes 2359300
  153.1 3.1 copy-start.2
  153.2 3.0 copy-start.59
  155.9 3.2 copy-start.10
  161.3 7.5 copy-start.32
  168.8 26.2 %copy-start.11 = (f32[512,768]{1,0:T(8,128)S(1)}, f32[512,768]{1,0:T(8,128)}, u32[]{:S(2)}) copy-start(f32[512,768]{1,0:T(8,128)} %copy-done.10) | copy-start | bytes 4718596
  195.0 6.5 slice-start
  195.0 6.5 slice-start.1
  201.1 3.7 slice-start.4
  202.3 2.6 slice-start.5
  202.3 7.8 slice-start.6
  204.9 5.1 copy-start.23
  204.9 5.1 slice-start.7
  210.0 2.8 copy-start.66
  212.8 18.5 %copy-start.8 = (f32[512,768]{1,0:T(8,128)}, f32[512,768]{1,0:T(8,128)S(1)}, u32[]{:S(2)}) copy-start(f32[512,768]{1,0:T(8,128)S(1)} %get-tuple-element.555) | copy-start | bytes 4718596
  226.5 4.8 copy-start.24
  226.5 4.8 copy-start.35
  226.5 11.9 %slice-start.2 = ((s8[6291456]{0:T(1024)(128)(4,1)}), s8[4194304]{0:T(1024)(128)(4,1)S(1)}, s32[]{:S(2)}) async-start(s8[6291456]{0:T(1024)(128)(4,1)} %bitcast.387), calls=%async_computation.18 | async-start | bytes 8388608
  231.3 7.1 slice-start.3
  248.5 4.8 copy-start.25
  248.5 4.8 copy-start.68
  248.5 4.8 copy-start.71
  253.3 8.5 copy-start.60
  368.2 3.1 copy-start.61
  374.8 92.1 %copy-start.41 = (f32[512,64]{0,1:T(8,128)S(1)}, f32[512,64]{0,1:T(8,128)}, u32[]{:S(2)}) copy-start(f32[512,64]{0,1:T(8,128)} %copy-done.40) | copy-start | bytes 393220
  475.7 4.5 copy-start.42
  475.7 4.5 copy-start.44
  475.7 4.6 copy-start.58
  491.2 3.4 copy-start.6
  491.3 88.9 %reduce-scatter.8.cloned.1.call-start = ((), (), s32[]{:S(2)}) async-start(), calls=%async_computation.10 | async-start | bytes 1327104 | tf_op jit(solution)/shard_map/reduce_scatter | solution.py:313
  492.4 2.3 copy-start.27
  496.5 6.3 copy-start.20
  496.6 141.4 %reduce-scatter.14.cloned.1.call-start = ((), (), s32[]{:S(2)}) async-start(), calls=%async_computation.13 | async-start | bytes 5308416 | tf_op jit(solution)/shard_map/reduce_scatter | solution.py:322
  496.8 6.1 copy-start.70
  508.3 5.9 copy-start.33
  508.3 186.9 %reduce-scatter.12.cloned.1.call-start = ((), (), s32[]{:S(2)}) async-start(), calls=%async_computation.12 | async-start | bytes 5308416 | tf_op jit(solution)/shard_map/reduce_scatter | solution.py:319
  509.4 4.8 copy-start.69
  518.8 234.0 %reduce-scatter.10.cloned.1.call-start = ((), (), s32[]{:S(2)}) async-start(), calls=%async_computation.11 | async-start | bytes 5308416 | tf_op jit(solution)/shard_map/reduce_scatter | solution.py:316
  519.1 4.8 copy-start.67
  528.5 330.0 %all-reduce.14.cloned.1.call-start = ((), (), s32[]{:S(2)}) async-start(), calls=%async_computation.15 | async-start | bytes 5013504 | tf_op jit(solution)/shard_map/psum | solution.py:350
  530.2 222.7 %copy-start.50 = (f32[768]{0:T(1024)S(1)}, f32[768]{0:T(1024)}, u32[]{:S(2)}) copy-start(f32[768]{0:T(1024)} %get-tuple-element.388) | copy-start | bytes 9220
  530.2 222.7 %copy-start.51 = (f32[768]{0:T(1024)S(1)}, f32[768]{0:T(1024)}, u32[]{:S(2)}) copy-start(f32[768]{0:T(1024)} %get-tuple-element.397) | copy-start | bytes 9220
  530.3 261.3 %copy-start.37 = (f32[512,768]{1,0:T(8,128)S(1)}, f32[512,768]{1,0:T(8,128)}, u32[]{:S(2)}) copy-start(f32[512,768]{1,0:T(8,128)} %copy-done.36) | copy-start | bytes 4718596
  791.6 4.9 copy-start.28
  791.6 4.9 copy-start.43
  791.6 4.9 copy-start.45
  791.6 4.9 copy-start.55
  858.5 2.3 copy-start.47
  858.5 3.4 copy-start.46
  (27 other events, 42.8 us)
Sparse Core Ops, SparseCore 0:
  9.9 36.8 all-gather.5
  48.7 24.0 all-gather.7
  74.6 38.9 all-gather.9
  115.3 38.9 all-gather.11
  156.0 38.9 all-gather.13
  491.4 48.0 reduce-scatter.15
  543.3 36.7 reduce-scatter.7
  583.9 53.9 reduce-scatter.13
  641.4 53.8 reduce-scatter.11
  698.9 53.8 reduce-scatter.9
  756.2 102.2 all-reduce.13
where the time goes:
time: 885 us; the launch traced here: 872 us
  matrix products  385 us (44%)
  waiting for transfers between devices  312 us (35%)
  local copies, waits for them, and re-layouts  64 us (7%)
  blocking collectives  51.8 us (6%)
  other arithmetic  39.6 us (4%)
  between operations  16.8 us (2%)
    dot_general x82, matrix products, times_transposed(): lax.dot_general(left_op, right_op, (((1,), (1,)), ((), ())), preferred_el...  147 us
    dot_general x58, matrix products, inner_sum(): lax.dot_general(left_op, right_op, (((0,), (0,)), ((), ())), preferred_el...  130 us
    dot_general x58, matrix products, matmul(): return jnp.dot(left_op, right_op, preferred_element_type=jnp.float32)  108 us
    reduce_scatter x1, waiting for transfers between devices, shards(): lax.psum_scatter(sum_down.astype(jnp.bfloat16), 'shard', scatter_dimensio...  57.8 us
    reduce_scatter x1, waiting for transfers between devices, shards(): lax.psum_scatter(sum_gate.astype(jnp.bfloat16), 'shard', scatter_dimensio...  57.6 us
    reduce_scatter x1, waiting for transfers between devices, shards(): lax.psum_scatter(sum_up.astype(jnp.bfloat16), 'shard', scatter_dimension=...  57.4 us
    psum x1, waiting for transfers between devices, shards(): lax.psum(part_qkv.astype(jnp.bfloat16), 'rep').astype(jnp.float32)  54.9 us
    unnamed x2, blocking collectives  39.4 us
  transfers between devices with their start and end apart: 11, of which 8 were waited for; matrix products, arithmetic and copies ran while one was open for 20% of the time, Pallas kernels for 0%

commit v1 on v0

v1 whole, which is shorter than its diff:
```python
import functools

import jax
import jax.numpy as jnp
from jax import lax
from jax.experimental import pallas as pl
from jax.experimental.pallas import tpu as pltpu
from jax.sharding import PartitionSpec as P

HEAD_DIM = 64
norm_eps = 1e-12
rope_base = 1000.0
masked_score = -1e30
f32 = jnp.float32
bf16 = jnp.bfloat16
ANY = pl.BlockSpec(memory_space=pl.ANY)
SMEM = pl.BlockSpec(memory_space=pltpu.SMEM)


def dot_nn(a, b):
    return lax.dot_general(a, b, (((1,), (0,)), ((), ())), preferred_element_type=f32)


def dot_nt(a, b):
    return lax.dot_general(a, b, (((1,), (1,)), ((), ())), preferred_element_type=f32)


def dot_tn(a, b):
    return lax.dot_general(a, b, (((0,), (0,)), ((), ())), preferred_element_type=f32)


def whole(shape):
    return pl.BlockSpec(shape, lambda *_: (0,) * len(shape))


def xor_permute(x, bit):
    count = lax.axis_size("shard")
    return lax.ppermute(x, "shard", [(i, i ^ bit) for i in range(count)])


def gather_pieces(own):
    count = lax.axis_size("shard")
    rows = own.shape[0]
    if count == 8:
        half = rows // 2
        from_x = xor_permute(own, 2)
        from_y = xor_permute(own, 4)
        far_a = xor_permute(from_y[:half], 2)
        far_b = xor_permute(from_x[half:], 4)
        pieces = [(0, 0, own), (2, 0, from_x), (4, 0, from_y), (6, 0, far_a), (6, half, far_b)]
    else:
        pieces = [(0, 0, own)]
        bit = 2
        while bit < count:
            pieces += [(r | bit, lo, xor_permute(p, bit)) for r, lo, p in pieces]
            bit *= 2
    return pieces + [(r | 1, lo, xor_permute(p, 1)) for r, lo, p in pieces]


def reduce_own(keep, send):
    held = keep + xor_permute(send, 1)
    parts = [held[0].astype(f32)]
    for q in range(1, held.shape[0]):
        parts.append(xor_permute(held[q], 2 * q).astype(f32))
    return functools.reduce(jnp.add, parts).astype(bf16)


def start_loads(metas, refs, me, shard_rows, dst, lo, cols, sems):
    copies = []
    for i, ((rel, first, rows), ref) in enumerate(zip(metas, refs)):
        at = (me ^ rel) * shard_rows + first
        copy = pltpu.make_async_copy(
            ref.at[:, pl.ds(lo, cols)],
            dst.at[pl.ds(pl.multiple_of(at, 8), rows), :],
            sems.at[i],
        )
        copy.start()
        copies.append(copy)
    return copies


def wait_all(copies):
    for copy in copies:
        copy.wait()


def metas_of(pieces):
    return tuple((rel, first, p.shape[0]) for rel, first, p in pieces)


def arrays_of(pieces):
    return [p for _, _, p in pieces]


def half_mask(shape):
    lane = lax.broadcasted_iota(jnp.int32, shape, len(shape) - 1)
    return (lane % HEAD_DIM) < HEAD_DIM // 2


def normalize(h):
    centre = h - jnp.mean(h, -1, keepdims=True)
    inv = lax.rsqrt(jnp.mean(centre * centre, -1, keepdims=True) + norm_eps)
    return centre * inv, inv


def norm_back(e, n, inv):
    return inv * (e - jnp.mean(e, -1, keepdims=True) - n * jnp.mean(e * n, -1, keepdims=True))


def qkv_kernel(metas, shard_rows, me_ref, x_ref, cos_ref, sin_ref, *rest):
    refs, (out_ref, w_ref, sems) = rest[: len(metas)], rest[len(metas) :]
    width = x_ref.shape[1]

    @pl.when(pl.program_id(0) == 0)
    def _():
        wait_all(start_loads(metas, refs, me_ref[0], shard_rows, w_ref, 0, w_ref.shape[1], sems))

    block = out_ref.shape[1]
    j = pl.program_id(0)
    lo = pl.multiple_of(j * block, block)
    y = dot_nn(x_ref[...], w_ref[:, pl.ds(lo, block)])

    @pl.when(lo < 2 * width)
    def _():
        rows, reps = cos_ref.shape[0], y.shape[0] // cos_ref.shape[0]
        first = half_mask((rows, 128))
        scale = jnp.where(lo < width, 0.125, 1.0).astype(f32)
        cos = cos_ref[...] * scale
        sin = sin_ref[...] * scale
        sin = jnp.where(first, -sin, sin)
        for s in range(reps):
            for b in range(block // 128):
                u = y[s * rows : (s + 1) * rows, b * 128 : (b + 1) * 128]
                turned = jnp.where(first, pltpu.roll(u, 96, 1), pltpu.roll(u, 32, 1))
                out_ref[s * rows : (s + 1) * rows, b * 128 : (b + 1) * 128] = (
                    u * cos + turned * sin
                ).astype(bf16)

    @pl.when(lo >= 2 * width)
    def _():
        out_ref[...] = y.astype(bf16)


def qkv_forward(me, tokens, cos, sin, pieces, shard_rows):
    rows, width = tokens.shape
    metas = metas_of(pieces)
    block = 256
    total = 3 * width
    return pl.pallas_call(
        functools.partial(qkv_kernel, metas, shard_rows),
        grid=(total // block,),
        in_specs=[SMEM, whole(tokens.shape), whole(cos.shape), whole(sin.shape)]
        + [ANY] * len(metas),
        out_specs=pl.BlockSpec((rows, block), lambda j: (0, j)),
        out_shape=jax.ShapeDtypeStruct((rows, total), bf16),
        scratch_shapes=[
            pltpu.VMEM((width, total), bf16),
            pltpu.SemaphoreType.DMA((len(metas),)),
        ],
        cost_estimate=pl.CostEstimate(
            flops=2 * rows * width * total, bytes_accessed=10_000_000, transcendentals=0
        ),
        name="qkv_rope",
    )(me, tokens, cos, sin, *arrays_of(pieces))


def attend_kernel(q_ref, k_ref, v_ref, row_ref, col_ref, o_ref, p_ref, bias_ref):
    @pl.when(pl.program_id(1) == 0)
    def _():
        bias_ref[...] = jnp.where(row_ref[0] == col_ref[0], 0.0, masked_score).astype(f32)

    heads = p_ref.shape[1]
    lane = lax.broadcasted_iota(jnp.int32, (1, 128), 1)
    for pair in range(heads // 2):
        cols = slice(pair * 128, (pair + 1) * 128)
        q, k, v = q_ref[:, cols], k_ref[:, cols], v_ref[:, cols]
        acc = None
        for side in range(2):
            mine = ((lane // HEAD_DIM) == side).astype(bf16)
            s = dot_nt(q, k * mine) + bias_ref[...]
            e = jnp.exp(s - jnp.max(s, -1, keepdims=True))
            inv = 1.0 / jnp.sum(e, -1, keepdims=True)
            p = (e * inv).astype(bf16)
            p_ref[0, pair * 2 + side] = p
            part = dot_nn(p, v * mine)
            acc = part if acc is None else acc + part
        o_ref[:, cols] = acc.astype(bf16)


def attend_forward(joint, seg_row, seg_col, width, quad=4):
    rows = joint.shape[0]
    seqs, _, seq = seg_row.shape
    lanes = quad * HEAD_DIM
    groups = width // lanes
    heads = width // HEAD_DIM
    spec = lambda part: pl.BlockSpec((seq, lanes), lambda s, g: (s, part * groups + g))
    return pl.pallas_call(
        attend_kernel,
        grid=(seqs, groups),
        in_specs=[
            spec(0),
            spec(1),
            spec(2),
            pl.BlockSpec((1, 1, seq), lambda s, g: (s, 0, 0)),
            pl.BlockSpec((1, seq, 1), lambda s, g: (s, 0, 0)),
        ],
        out_specs=[
            pl.BlockSpec((seq, lanes), lambda s, g: (s, g)),
            pl.BlockSpec((1, quad, seq, seq), lambda s, g: (s, g, 0, 0)),
        ],
        out_shape=[
            jax.ShapeDtypeStruct((rows, width), bf16),
            jax.ShapeDtypeStruct((seqs, heads, seq, seq), bf16),
        ],
        scratch_shapes=[pltpu.VMEM((seq, seq), f32)],
        cost_estimate=pl.CostEstimate(
            flops=4 * seqs * heads * seq * seq * 256,
            bytes_accessed=20_000_000,
            transcendentals=seqs * heads * seq * seq,
        ),
        name="attend_fwd",
    )(joint, joint, joint, seg_row, seg_col)


def out_kernel(metas, shard_rows, lo, me_ref, att_ref, x_ref, *rest):
    refs = rest[: len(metas)]
    n1_ref, inv_ref, low_ref, vec_ref, w_ref, v_ref, sems = rest[len(metas) :]
    width = x_ref.shape[1]

    @pl.when(pl.program_id(0) == 0)
    def _():
        me = me_ref[0]
        copies = start_loads(metas, refs, me, shard_rows, w_ref, lo, width, sems.at[0])
        copies += start_loads(metas, refs, me, shard_rows, v_ref, lo + width, 128, sems.at[1])
        wait_all(copies)
        eye = (
            lax.broadcasted_iota(jnp.int32, (8, 128), 0)
            == lax.broadcasted_iota(jnp.int32, (8, 128), 1)
        ).astype(bf16)
        vec_ref[...] = dot_nt(eye, v_ref[...])

    h = x_ref[...].astype(f32) + dot_nn(att_ref[...], w_ref[...])
    n, inv = normalize(h)
    n1_ref[...] = n
    inv_ref[...] = jnp.broadcast_to(inv, inv_ref.shape)
    low_ref[...] = (n * vec_ref[0:1] + vec_ref[1:2]).astype(bf16)


def out_forward(me, attended, tokens, pieces, shard_rows):
    rows, width = tokens.shape
    metas = metas_of(pieces)
    block = 512
    by_row = lambda cols: pl.BlockSpec((block, cols), lambda i: (i, 0))
    return pl.pallas_call(
        functools.partial(out_kernel, metas, shard_rows, 3 * width),
        grid=(rows // block,),
        in_specs=[SMEM, by_row(width), by_row(width)] + [ANY] * len(metas),
        out_specs=[by_row(width), by_row(128), by_row(width), whole((8, width))],
        out_shape=[
            jax.ShapeDtypeStruct((rows, width), f32),
            jax.ShapeDtypeStruct((rows, 128), f32),
            jax.ShapeDtypeStruct((rows, width), bf16),
            jax.ShapeDtypeStruct((8, width), f32),
        ],
        scratch_shapes=[
            pltpu.VMEM((width, width), bf16),
            pltpu.VMEM((width, 128), bf16),
            pltpu.SemaphoreType.DMA((2, len(metas))),
        ],
        cost_estimate=pl.CostEstimate(
            flops=2 * rows * width * width, bytes_accessed=12_000_000, transcendentals=rows
        ),
        name="out_norm",
    )(me, attended, tokens, *arrays_of(pieces))


def gate_kernel(metas, shard_rows, me_ref, x_ref, *rest):
    refs, (h_ref, a_ref, b_ref, w_ref, sems) = rest[: len(metas)], rest[len(metas) :]

    @pl.when(pl.program_id(0) == 0)
    def _():
        wait_all(start_loads(metas, refs, me_ref[0], shard_rows, w_ref, 0, w_ref.shape[1], sems))

    hidden = w_ref.shape[1] // 2
    block = h_ref.shape[1]
    sub = 256
    x = x_ref[...]
    for c in range(block // sub):
        lo = pl.multiple_of(pl.program_id(0) * block + c * sub, sub)
        gate = dot_nn(x, w_ref[:, pl.ds(lo, sub)])
        up = dot_nn(x, w_ref[:, pl.ds(pl.multiple_of(hidden + lo, sub), sub)])
        s = 0.5 * jnp.tanh(0.5 * gate) + 0.5
        act = gate * s
        cols = slice(c * sub, (c + 1) * sub)
        h_ref[:, cols] = (act * up).astype(bf16)
        b_ref[:, cols] = act.astype(bf16)
        a_ref[:, cols] = (up * s * (1.0 + gate * (1.0 - s))).astype(bf16)


def gate_forward(me, low, pieces, shard_rows, hidden):
    rows, width = low.shape
    metas = metas_of(pieces)
    block = 768
    spec = pl.BlockSpec((rows, block), lambda j: (0, j))
    shape = jax.ShapeDtypeStruct((rows, hidden), bf16)
    return pl.pallas_call(
        functools.partial(gate_kernel, metas, shard_rows),
        grid=(hidden // block,),
        in_specs=[SMEM, whole(low.shape)] + [ANY] * len(metas),
        out_specs=[spec] * 3,
        out_shape=[shape] * 3,
        scratch_shapes=[
            pltpu.VMEM((width, 2 * hidden), bf16),
            pltpu.SemaphoreType.DMA((len(metas),)),
        ],
        cost_estimate=pl.CostEstimate(
            flops=4 * rows * width * hidden,
            bytes_accessed=30_000_000,
            transcendentals=rows * hidden,
        ),
        name="gate_up",
    )(me, low, *arrays_of(pieces))


def down_kernel(metas, shard_rows, me_ref, h_ref, n1_ref, cot_ref, vec_ref, *rest):
    refs = rest[: len(metas)]
    out_ref, g2_ref, g2low_ref, sums_ref, w_ref, sems = rest[len(metas) :]

    @pl.when(pl.program_id(0) == 0)
    def _():
        wait_all(start_loads(metas, refs, me_ref[0], shard_rows, w_ref, 0, w_ref.shape[1], sems))
        sums_ref[...] = jnp.zeros_like(sums_ref)

    mixed = n1_ref[...] * vec_ref[0:1] + vec_ref[1:2]
    n, inv = normalize(mixed + dot_nn(h_ref[...], w_ref[...]))
    out_ref[...] = (n * vec_ref[2:3] + vec_ref[3:4]).astype(bf16)
    cot = cot_ref[...].astype(f32)
    sums_ref[0:1] += jnp.sum(cot * n, 0, keepdims=True)
    sums_ref[1:2] += jnp.sum(cot, 0, keepdims=True)
    g = norm_back(cot * vec_ref[2:3], n, inv)
    g2_ref[...] = g
    g2low_ref[...] = g.astype(bf16)


def down_forward(me, hidden_low, n1, cot, vec, pieces, shard_rows):
    rows, hidden = hidden_low.shape
    width = n1.shape[1]
    metas = metas_of(pieces)
    block = 256
    by_row = lambda cols: pl.BlockSpec((block, cols), lambda i: (i, 0))
    return pl.pallas_call(
        functools.partial(down_kernel, metas, shard_rows),
        grid=(rows // block,),
        in_specs=[SMEM, by_row(hidden), by_row(width), by_row(width), whole(vec.shape)]
        + [ANY] * len(metas),
        out_specs=[by_row(width), by_row(width), by_row(width), whole((8, width))],
        out_shape=[
            jax.ShapeDtypeStruct((rows, width), bf16),
            jax.ShapeDtypeStruct((rows, width), f32),
            jax.ShapeDtypeStruct((rows, width), bf16),
            jax.ShapeDtypeStruct((8, width), f32),
        ],
        scratch_shapes=[
            pltpu.VMEM((hidden, width), bf16),
            pltpu.SemaphoreType.DMA((len(metas),)),
        ],
        cost_estimate=pl.CostEstimate(
            flops=2 * rows * width * hidden, bytes_accessed=20_000_000, transcendentals=rows
        ),
        name="down_norm",
    )(me, hidden_low, n1, cot, vec, *arrays_of(pieces))


def down_grad_kernel(me_ref, h_ref, g_ref, keep_ref, send_ref, acc_ref):
    rows = keep_ref.shape[1]
    core = me_ref[0] & 1
    acc_ref[...] = dot_tn(h_ref[...], g_ref[...])
    keep_ref[0] = acc_ref[pl.ds(pl.multiple_of(core * rows, 8), rows), :].astype(bf16)
    send_ref[0] = acc_ref[pl.ds(pl.multiple_of((1 - core) * rows, 8), rows), :].astype(bf16)


def down_grad(me, hidden_low, g2low, chips):
    rows, hidden = hidden_low.shape
    width = g2low.shape[1]
    per_chip = hidden // chips
    shape = jax.ShapeDtypeStruct((chips, per_chip // 2, width), bf16)
    spec = pl.BlockSpec((1, per_chip // 2, width), lambda q, me: (q, 0, 0))
    return pl.pallas_call(
        down_grad_kernel,
        grid_spec=pltpu.PrefetchScalarGridSpec(
            num_scalar_prefetch=1,
            grid=(chips,),
            in_specs=[
                pl.BlockSpec((rows, per_chip), lambda q, me: (0, (me[0] // 2) ^ q)),
                pl.BlockSpec((rows, width), lambda q, me: (0, 0)),
            ],
            out_specs=[spec, spec],
            scratch_shapes=[pltpu.VMEM((per_chip, width), f32)],
        ),
        out_shape=[shape, shape],
        cost_estimate=pl.CostEstimate(
            flops=2 * rows * width * hidden, bytes_accessed=13_000_000, transcendentals=0
        ),
        name="down_grad",
    )(me, hidden_low, g2low)


def spread(me, acc_ref, keep_ref, send_ref, cols):
    rows = keep_ref.shape[1]
    chip, core = me // 2, me & 1
    for q in range(keep_ref.shape[0]):
        base = (chip ^ q) * 2
        keep_ref[q, :, cols] = acc_ref[
            pl.ds(pl.multiple_of((base + core) * rows, 8), rows), :
        ].astype(bf16)
        send_ref[q, :, cols] = acc_ref[
            pl.ds(pl.multiple_of((base + 1 - core) * rows, 8), rows), :
        ].astype(bf16)


def hidden_grad_kernel(metas, shard_rows, me_ref, g_ref, a_ref, b_ref, *rest):
    refs, (gg_ref, gu_ref, w_ref, sems) = rest[: len(metas)], rest[len(metas) :]

    @pl.when(pl.program_id(0) == 0)
    def _():
        wait_all(start_loads(metas, refs, me_ref[0], shard_rows, w_ref, 0, w_ref.shape[1], sems))

    block = gg_ref.shape[1]
    sub = 256
    for c in range(block // sub):
        lo = pl.multiple_of(pl.program_id(0) * block + c * sub, sub)
        gh = dot_nt(g_ref[...], w_ref[pl.ds(lo, sub), :])
        cols = slice(c * sub, (c + 1) * sub)
        gg_ref[:, cols] = (gh * a_ref[:, cols].astype(f32)).astype(bf16)
        gu_ref[:, cols] = (gh * b_ref[:, cols].astype(f32)).astype(bf16)


def hidden_grad(me, g2low, a, b, pieces, shard_rows):
    rows, hidden = a.shape
    width = g2low.shape[1]
    metas = metas_of(pieces)
    block = 768
    spec = pl.BlockSpec((rows, block), lambda j: (0, j))
    shape = jax.ShapeDtypeStruct((rows, hidden), bf16)
    return pl.pallas_call(
        functools.partial(hidden_grad_kernel, metas, shard_rows),
        grid=(hidden // block,),
        in_specs=[SMEM, whole(g2low.shape), spec, spec] + [ANY] * len(metas),
        out_specs=[spec, spec],
        out_shape=[shape, shape],
        scratch_shapes=[
            pltpu.VMEM((hidden, width), bf16),
            pltpu.SemaphoreType.DMA((len(metas),)),
        ],
        cost_estimate=pl.CostEstimate(
            flops=2 * rows * width * hidden, bytes_accessed=32_000_000, transcendentals=0
        ),
        name="hidden_grad",
    )(me, g2low, a, b, *arrays_of(pieces))


def weight_grad_kernel(me_ref, x_ref, g_ref, keep_ref, send_ref, acc_ref):
    acc_ref[...] = dot_tn(x_ref[...], g_ref[...])
    spread(me_ref[0], acc_ref, keep_ref, send_ref, slice(None))


def weight_grad(me, x, g, count, name, block=768):
    rows, width = x.shape
    cols = g.shape[1]
    chips, shard_rows = count // 2, width // count
    shape = jax.ShapeDtypeStruct((chips, shard_rows, cols), bf16)
    spec = pl.BlockSpec((chips, shard_rows, block), lambda j: (0, 0, j))
    return pl.pallas_call(
        weight_grad_kernel,
        grid=(cols // block,),
        in_specs=[SMEM, whole(x.shape), pl.BlockSpec((rows, block), lambda j: (0, j))],
        out_specs=[spec, spec],
        out_shape=[shape, shape],
        scratch_shapes=[pltpu.VMEM((width, block), f32)],
        cost_estimate=pl.CostEstimate(
            flops=2 * rows * width * cols, bytes_accessed=13_000_000, transcendentals=0
        ),
        name=name,
    )(me, x, g)


def mixed_grad_kernel(
    metas, metas_out, shard_rows, out_lo,
    me_ref, gg_ref, gu_ref, g2_ref, n1_ref, inv_ref, vec_ref, *rest,
):
    refs, rest = rest[: len(metas)], rest[len(metas) :]
    refs_out, rest = rest[: len(metas_out)], rest[len(metas_out) :]
    g1_ref, g1low_ref, gatt_ref, sums_ref, w_ref, wo_ref, sems, sems_out = rest
    width = g1_ref.shape[1]
    hidden = w_ref.shape[1] // 2

    @pl.when(pl.program_id(0) == 0)
    def _():
        me = me_ref[0]
        copies = start_loads(metas, refs, me, shard_rows, w_ref, 0, 2 * hidden, sems)
        copies += start_loads(metas_out, refs_out, me, shard_rows, wo_ref, out_lo, width, sems_out)
        wait_all(copies)
        sums_ref[...] = jnp.zeros_like(sums_ref)

    gm = (
        g2_ref[...]
        + dot_nt(gg_ref[...], w_ref[:, :hidden])
        + dot_nt(gu_ref[...], w_ref[:, hidden:])
    )
    n = n1_ref[...]
    sums_ref[0:1] += jnp.sum(gm * n, 0, keepdims=True)
    sums_ref[1:2] += jnp.sum(gm, 0, keepdims=True)
    g = norm_back(gm * vec_ref[0:1], n, inv_ref[:, 0:1])
    g1_ref[...] = g
    low = g.astype(bf16)
    g1low_ref[...] = low
    gatt_ref[...] = dot_nt(low, wo_ref[...]).astype(bf16)


def mixed_grad(me, gg, gu, g2, n1, inv1, vec, pieces, pieces_out, shard_rows):
    rows, hidden = gg.shape
    width = g2.shape[1]
    metas, metas_out = metas_of(pieces), metas_of(pieces_out)
    block = 256
    by_row = lambda cols: pl.BlockSpec((block, cols), lambda i: (i, 0))
    return pl.pallas_call(
        functools.partial(mixed_grad_kernel, metas, metas_out, shard_rows, 3 * width),
        grid=(rows // block,),
        in_specs=[
            SMEM, by_row(hidden), by_row(hidden), by_row(width), by_row(width), by_row(128),
            whole(vec.shape),
        ]
        + [ANY] * (len(metas) + len(metas_out)),
        out_specs=[by_row(width), by_row(width), by_row(width), whole((8, width))],
        out_shape=[
            jax.ShapeDtypeStruct((rows, width), f32),
            jax.ShapeDtypeStruct((rows, width), bf16),
            jax.ShapeDtypeStruct((rows, width), bf16),
            jax.ShapeDtypeStruct((8, width), f32),
        ],
        scratch_shapes=[
            pltpu.VMEM((width, 2 * hidden), bf16),
            pltpu.VMEM((width, width), bf16),
            pltpu.SemaphoreType.DMA((len(metas),)),
            pltpu.SemaphoreType.DMA((len(metas_out),)),
        ],
        cost_estimate=pl.CostEstimate(
            flops=4 * rows * width * hidden + 2 * rows * width * width,
            bytes_accessed=36_000_000,
            transcendentals=0,
        ),
        name="mixed_grad",
    )(me, gg, gu, g2, n1, inv1, vec, *arrays_of(pieces), *arrays_of(pieces_out))


def up_out_grad_kernel(me_ref, x_ref, g_ref, att_ref, g1_ref, s2_ref, s1_ref, keep_ref, send_ref, acc_ref):
    me = me_ref[0]
    width = x_ref.shape[1]
    cols = g_ref.shape[1]
    for j in range(cols // width):
        acc_ref[...] = dot_tn(x_ref[...], g_ref[:, j * width : (j + 1) * width])
        spread(me, acc_ref, keep_ref, send_ref, slice(j * width, (j + 1) * width))
    acc_ref[...] = dot_tn(att_ref[...], g1_ref[...])
    spread(me, acc_ref, keep_ref, send_ref, slice(cols, cols + width))
    row = lax.broadcasted_iota(jnp.int32, (8, width), 0)
    rows = jnp.where(row < 2, s2_ref[...], pltpu.roll(s1_ref[...], 2, 0)).astype(bf16)
    eye = (
        lax.broadcasted_iota(jnp.int32, (8, 128), 0) == lax.broadcasted_iota(jnp.int32, (8, 128), 1)
    ).astype(bf16)
    acc_ref[:, :128] = dot_tn(rows, eye)
    spread(me, acc_ref.at[:, :128], keep_ref, send_ref, slice(cols + width, cols + width + 128))


def up_out_grad(me, low, gu, attended, g1low, sums2, sums1, count):
    rows, width = low.shape
    cols = gu.shape[1]
    chips, shard_rows = count // 2, width // count
    total = cols + width + 128
    shape = jax.ShapeDtypeStruct((chips, shard_rows, total), bf16)
    vmem = pl.BlockSpec(memory_space=pltpu.VMEM)
    return pl.pallas_call(
        up_out_grad_kernel,
        in_specs=[SMEM] + [vmem] * 6,
        out_specs=[vmem, vmem],
        out_shape=[shape, shape],
        scratch_shapes=[pltpu.VMEM((width, width), f32)],
        cost_estimate=pl.CostEstimate(
            flops=2 * rows * width * (cols + width), bytes_accessed=16_000_000, transcendentals=0
        ),
        name="up_out_grad",
    )(me, low, gu, attended, g1low, sums2, sums1)


def attend_back_kernel(q_ref, k_ref, v_ref, o_ref, g_ref, p_ref, cos_ref, sin_ref, dq_ref, dk_ref, dv_ref):
    heads = p_ref.shape[1]
    lane = lax.broadcasted_iota(jnp.int32, (1, 128), 1)
    first = half_mask((cos_ref.shape[0], 128))
    cos, sin = cos_ref[...], sin_ref[...]

    def unrotate(g):
        t = g * sin
        return g * cos + jnp.where(first, pltpu.roll(t, 96, 1), -pltpu.roll(t, 32, 1))

    for pair in range(heads // 2):
        cols = slice(pair * 128, (pair + 1) * 128)
        q, k, v, g = q_ref[:, cols], k_ref[:, cols], v_ref[:, cols], g_ref[:, cols]
        go = g.astype(f32) * o_ref[:, cols].astype(f32)
        dq = dk = dv = None
        for side in range(2):
            mine = (lane // HEAD_DIM) == side
            keep = mine.astype(bf16)
            p = p_ref[0, pair * 2 + side]
            row = jnp.sum(jnp.where(mine, go, 0.0), -1, keepdims=True)
            gp = dot_nt(g, v * keep)
            gs = (p.astype(f32) * (gp - row)).astype(bf16)
            parts = (dot_nn(gs, k * keep), dot_tn(gs, q * keep), dot_tn(p, g * keep))
            if dq is None:
                dq, dk, dv = parts
            else:
                dq, dk, dv = dq + parts[0], dk + parts[1], dv + parts[2]
        dq_ref[:, cols] = unrotate(dq * 0.125).astype(bf16)
        dk_ref[:, cols] = unrotate(dk).astype(bf16)
        dv_ref[:, cols] = dv.astype(bf16)


def attend_backward(joint, attended, gatt, probs, cos, sin):
    rows, width = attended.shape
    seqs, heads, seq, _ = probs.shape
    quad = 4
    lanes = quad * HEAD_DIM
    groups = width // lanes
    spec = lambda part: pl.BlockSpec((seq, lanes), lambda s, g: (s, part * groups + g))
    shape = jax.ShapeDtypeStruct((rows, width), bf16)
    return pl.pallas_call(
        attend_back_kernel,
        grid=(seqs, groups),
        in_specs=[
            spec(0), spec(1), spec(2), spec(0), spec(0),
            pl.BlockSpec((1, quad, seq, seq), lambda s, g: (s, g, 0, 0)),
            pl.BlockSpec(cos.shape, lambda s, g: (0, 0)),
            pl.BlockSpec(sin.shape, lambda s, g: (0, 0)),
        ],
        out_specs=[spec(0)] * 3,
        out_shape=[shape] * 3,
        cost_estimate=pl.CostEstimate(
            flops=8 * seqs * heads * seq * seq * 256, bytes_accessed=25_000_000, transcendentals=0
        ),
        name="attend_bwd",
    )(joint, joint, joint, attended, gatt, probs, cos, sin)


def qkv_grad_kernel(me_ref, x_ref, dq_ref, dk_ref, dv_ref, keep_ref, send_ref, acc_ref):
    width = x_ref.shape[1]
    for j, ref in enumerate((dq_ref, dk_ref, dv_ref)):
        acc_ref[...] = dot_tn(x_ref[...], ref[...])
        spread(me_ref[0], acc_ref, keep_ref, send_ref, slice(j * width, (j + 1) * width))


def qkv_grad(me, tokens, dq, dk, dv, count):
    rows, width = tokens.shape
    chips, shard_rows = count // 2, width // count
    shape = jax.ShapeDtypeStruct((chips, shard_rows, 3 * width), bf16)
    vmem = pl.BlockSpec(memory_space=pltpu.VMEM)
    return pl.pallas_call(
        qkv_grad_kernel,
        in_specs=[SMEM] + [vmem] * 4,
        out_specs=[vmem, vmem],
        out_shape=[shape, shape],
        scratch_shapes=[pltpu.VMEM((width, width), f32)],
        cost_estimate=pl.CostEstimate(
            flops=6 * rows * width * width, bytes_accessed=10_000_000, transcendentals=0
        ),
        name="qkv_grad",
    )(me, tokens, dq, dk, dv)


def input_grad_kernel(metas, shard_rows, me_ref, g1_ref, dq_ref, dk_ref, dv_ref, *rest):
    refs, (out_ref, w_ref, sems) = rest[: len(metas)], rest[len(metas) :]
    width = out_ref.shape[1]

    @pl.when(pl.program_id(0) == 0)
    def _():
        wait_all(start_loads(metas, refs, me_ref[0], shard_rows, w_ref, 0, 3 * width, sems))

    total = g1_ref[...]
    for j, ref in enumerate((dq_ref, dk_ref, dv_ref)):
        total += dot_nt(ref[...], w_ref[:, j * width : (j + 1) * width])
    out_ref[...] = total.astype(bf16)


def input_grad(me, g1, dq, dk, dv, pieces, shard_rows):
    rows, width = g1.shape
    metas = metas_of(pieces)
    block = 512
    by_row = pl.BlockSpec((block, width), lambda i: (i, 0))
    return pl.pallas_call(
        functools.partial(input_grad_kernel, metas, shard_rows),
        grid=(rows // block,),
        in_specs=[SMEM] + [by_row] * 4 + [ANY] * len(metas),
        out_specs=by_row,
        out_shape=jax.ShapeDtypeStruct((rows, width), bf16),
        scratch_shapes=[
            pltpu.VMEM((width, 3 * width), bf16),
            pltpu.SemaphoreType.DMA((len(metas),)),
        ],
        cost_estimate=pl.CostEstimate(
            flops=6 * rows * width * width, bytes_accessed=14_000_000, transcendentals=0
        ),
        name="input_grad",
    )(me, g1, dq, dk, dv, *arrays_of(pieces))


def rope_tables(seq_len):
    places = jnp.arange(seq_len, dtype=jnp.int32).astype(f32)
    frequency = rope_base ** (-jnp.arange(0, HEAD_DIM, 2, dtype=f32) / HEAD_DIM)
    angles = places[:, None] * frequency[None, :]
    return (jnp.tile(jnp.cos(angles), (1, 4)), jnp.tile(jnp.sin(angles), (1, 4)))


def shards(
    tokens, segment_ids, qkv_weight, out_weight, gate_weight, up_weight, down_weight,
    norm1_gain, norm1_bias, norm2_gain, norm2_bias, out_grad,
):
    count = lax.axis_size("shard")
    me = lax.axis_index("shard").astype(jnp.int32).reshape(1)
    batches, seq, width = tokens.shape
    shard_rows = qkv_weight.shape[0]
    hidden = gate_weight.shape[1]
    rows = batches * seq

    vectors = jnp.stack([norm1_gain, norm1_bias, norm2_gain, norm2_bias], 1)
    vectors = jnp.pad(vectors, ((0, 0), (0, 124)))
    pieces_a = gather_pieces(jnp.concatenate([qkv_weight, out_weight, vectors], 1))
    pieces_b = gather_pieces(jnp.concatenate([gate_weight, up_weight], 1))
    pieces_c = gather_pieces(down_weight)

    x = tokens.reshape(rows, width)
    cos, sin = rope_tables(seq)
    seg = segment_ids.reshape(batches, 1, seq)
    seg_col = segment_ids.reshape(batches, seq, 1)

    joint = qkv_forward(me, x, cos, sin, pieces_a, shard_rows)
    attended, probs = attend_forward(joint, seg, seg_col, width)
    n1, inv1, low, vec = out_forward(me, attended, x, pieces_a, shard_rows)
    hidden_low, back_gate, back_up = gate_forward(me, low, pieces_b, shard_rows, hidden)
    output, g2, g2low, sums2 = down_forward(
        me, hidden_low, n1, out_grad.reshape(rows, width), vec, pieces_c, down_weight.shape[0]
    )

    down_part = reduce_own(*down_grad(me, hidden_low, g2low, count // 2))
    gg, gu = hidden_grad(me, g2low, back_gate, back_up, pieces_c, down_weight.shape[0])
    gate_part = reduce_own(*weight_grad(me, low, gg, count, "gate_grad"))
    g1, g1low, gatt, sums1 = mixed_grad(
        me, gg, gu, g2, n1, inv1, vec, pieces_b, pieces_a, shard_rows
    )
    up_part = reduce_own(*up_out_grad(me, low, gu, attended, g1low, sums2, sums1, count))
    dq, dk, dv = attend_backward(joint, attended, gatt, probs, cos, sin)
    qkv_part = reduce_own(*qkv_grad(me, x, dq, dk, dv, count))
    in_grad = input_grad(me, g1, dq, dk, dv, pieces_a, shard_rows)

    total = lambda part: lax.psum(part, "rep").astype(f32)
    down_sum, gate_sum, up_sum, qkv_sum = map(total, (down_part, gate_part, up_part, qkv_part))
    vec_sum = up_sum[:, hidden + width :]
    return (
        output.reshape(tokens.shape),
        in_grad.reshape(tokens.shape),
        qkv_sum,
        up_sum[:, hidden : hidden + width],
        gate_sum,
        up_sum[:, :hidden],
        down_sum,
        vec_sum[:, 2],
        vec_sum[:, 3],
        vec_sum[:, 0],
        vec_sum[:, 1],
    )


def solution(mesh):
    rows3 = P(None, ("shard", "rep"), None)
    rows2 = P("shard", None)
    rows1 = P("shard")
    in_specs = (rows3, P(None, ("shard", "rep"))) + (rows2,) * 5 + (rows1,) * 4 + (rows3,)
    out_specs = (rows3, rows3) + (rows2,) * 5 + (rows1,) * 4
    return jax.shard_map(shards, mesh=mesh, in_specs=in_specs, out_specs=out_specs, check_vma=False)
```

time: 885 us -> 510 us (0.58); the launches traced: 872 us -> 506 us
  matrix products: 385 us -> 0 us
  Pallas kernels: 0 us -> 185 us
  waiting for transfers between devices: 312 us -> 244 us
  local copies, waits for them, and re-layouts: 64 us -> 10.8 us
  blocking collectives: 51.8 us -> 0 us
  starting transfers between devices: 0.9 us -> 34.6 us
  other arithmetic: 39.6 us -> 17.5 us
    dot_general x198 -> x0, matrix products: 385 us -> none  [the longest x82 147 us: times_transposed(): lax.dot_general(left_op, right_op, (((1,), (1,)), ((), ())), preferred_el...]
    reduce_scatter x4 -> x0, waiting for transfers between devices: 211 us -> none  [the longest x1 57.8 us: shards(): lax.psum_scatter(sum_down.astype(jnp.bfloat16), 'shard', scatter_dimensio...]
    pallas_call x0 -> x13, Pallas kernels: none -> 185 us  [the longest x1 24.1 us: mixed_grad(): pl.pallas_call(functools.partial(mixed_grad_kernel, metas, metas_out, sha...]
    ppermute x0 -> x43, waiting for transfers between devices: none -> 155 us  [xor_permute(): return lax.ppermute(x, 'shard', [(i, i ^ bit) for i in range(count)])]
    unnamed x2 -> x0, blocking collectives: 39.4 us -> none
    unnamed x184 -> x65, local copies, waits for them, and re-layouts: 39.2 us -> 2.27 us
    ppermute x0 -> x43, starting transfers between devices: none -> 34.6 us  [xor_permute(): return lax.ppermute(x, 'shard', [(i, i ^ bit) for i in range(count)])]
    psum x1, waiting for transfers between devices: 54.9 us -> 88.6 us  [shards(): total = lambda part: lax.psum(part, 'rep').astype(f32)]
  transfers between devices with their start and end apart: 11 -> 44, of which waited for: 8 -> 14; matrix products, arithmetic and copies ran while one was open for 20% -> 3% of each run, Pallas kernels for 0% -> 20%
where the time goes in v1:
time: 510 us; the launch traced here: 506 us
  waiting for transfers between devices  244 us (48%)
  Pallas kernels  185 us (36%)
  starting transfers between devices  34.6 us (7%)
  other arithmetic  17.5 us (3%)
  between operations  14.8 us (3%)
  local copies, waits for them, and re-layouts  10.8 us (2%)
    ppermute x43, waiting for transfers between devices, xor_permute(): return lax.ppermute(x, 'shard', [(i, i ^ bit) for i in range(count)])  155 us
    psum x1, waiting for transfers between devices, shards(): total = lambda part: lax.psum(part, 'rep').astype(f32)  88.6 us
    ppermute x43, starting transfers between devices, xor_permute(): return lax.ppermute(x, 'shard', [(i, i ^ bit) for i in range(count)])  34.6 us
    pallas_call x1, Pallas kernels, mixed_grad(): pl.pallas_call(functools.partial(mixed_grad_kernel, metas, metas_out, sha...  24.1 us
    pallas_call x1, Pallas kernels, attend_backward(): pl.pallas_call(attend_back_kernel, grid=(seqs, groups), in_specs=[spec(0)...  20.6 us
    pallas_call x1, Pallas kernels, gate_forward(): pl.pallas_call(functools.partial(gate_kernel, metas, shard_rows), grid=(h...  19.8 us
    pallas_call x1, Pallas kernels, attend_forward(): pl.pallas_call(attend_kernel, grid=(seqs, groups), in_specs=[spec(0), spe...  17.3 us
    pallas_call x1, Pallas kernels, hidden_grad(): pl.pallas_call(functools.partial(hidden_grad_kernel, metas, shard_rows),...  15.8 us
  transfers between devices with their start and end apart: 44, of which 14 were waited for; matrix products, arithmetic and copies ran while one was open for 3% of the time, Pallas kernels for 20%

profile of v1, /device:TPU:0, one launch (start us, length us, event | category | flops | bytes accessed | tf_op | source)
XLA Modules:
  0.0 506.2 jit_solution(10671989455255640929)
XLA Ops:
  7.2 0.8 pad_maximum_fusion
  8.2 1.2 fusion.13.rest_0_.rest_10_
  9.4 3.0 collective-permute-start.1
  12.6 2.0 collective-permute-start.10
  14.6 1.5 collective-permute-start
  16.7 23.1 %collective-permute-done.19.rest_2_ = bf16[384,768]{1,0:T(8,128)(2,1)S(1)} collective-permute-done((bf16[384,768]{1,0:T(8,128)(2,1)}, bf16[384,768]{1,0:T(8,128)(2,1)S(1)}, u32[]{:S(2)}, u32[]{:S(2)}) %collective-permute-start.19) | collective-permute-done | bytes 589856 | tf_op jit(solution)/shard_map/ppermute | solution.py:38
  39.7 2.0 collective-permute-start.9
  41.8 1.4 collective-permute-done.18.rest_1_
  43.2 1.6 collective-permute-start.2
  45.7 34.5 %collective-permute-done.20.rest_3_ = bf16[192,768]{1,0:T(8,128)(2,1)S(1)} collective-permute-done((bf16[192,768]{1,0:T(8,128)(2,1)S(1)}, bf16[192,768]{1,0:T(8,128)(2,1)S(1)}, u32[]{:S(2)}, u32[]{:S(2)}) %collective-permute-start.20) | collective-permute-done | bytes 294944 | tf_op jit(solution)/shard_map/ppermute | solution.py:38
  81.7 1.0 slice.119
  82.6 0.9 slice.120
  83.5 7.0 %collective-permute-done.21.rest_4_ = bf16[192,768]{1,0:T(8,128)(2,1)S(1)} collective-permute-done((bf16[192,768]{1,0:T(8,128)(2,1)S(1)}, bf16[192,768]{1,0:T(8,128)(2,1)S(1)}, u32[]{:S(2)}, u32[]{:S(2)}) %collective-permute-start.21) | collective-permute-done | bytes 294944 | tf_op jit(solution)/shard_map/ppermute | solution.py:38
  90.5 1.5 collective-permute-start.11
  92.0 0.7 copy-done.15
  94.3 0.9 copy.37.cos_ref
  95.2 0.8 copy.38.sin_ref
  96.6 1.0 copy.39.col_ref
  97.6 14.3 %qkv_rope.1.q_ref.k_ref.v_ref = bf16[1024,2304]{1,0:T(8,128)(2,1)} custom-call(s32[1]{0:T(128)} %bitcast.me_ref, bf16[1024,768]{1,0:T(8,128)(2,1)} %bitcast.56, f32[512,128]{1,0:T(8,128)} %copy.37.cos_ref, f32[512,128]{1,0:T(8,128)} %copy.38.sin_ref, bf16[96,3200]{1,0:T(8,128)(2,1)} %copy-done.1, bf16[96,3200]{1,0:T(8,128)(2,1)} %copy-done.3, ...), custom_call_target="tpu_custom_call" | custom-call | flops 3623878656 | bytes 10000000 | tf_op jit(solution)/shard_map/qkv_rope/pallas_call | solution.py:149
  112.5 17.3 %attend_fwd.1 = (bf16[1024,768]{1,0:T(8,128)(2,1)}, bf16[2,12,512,512]{3,2,1,0:T(8,128)(2,1)}) custom-call(bf16[1024,2304]{1,0:T(8,128)(2,1)} %qkv_rope.1.q_ref.k_ref.v_ref, bf16[1024,2304]{1,0:T(8,128)(2,1)} %qkv_rope.1.q_ref.k_ref.v_ref, bf16[1024,2304]{1,0:T(8,128)(2,1)} %qkv_rope.1.q_ref.k_ref.v_ref, s32[2,1,512]{2,1,0:T(1,128)} %reshape.123.row_ref, ...), custom_call_target="tpu_custom_call" | custom-call | flops 6442450944 | bytes 20000000 | tf_op jit(solution)/shard_map/attend_fwd/pallas_call | solution.py:197
  129.9 7.2 %out_norm.1 = (f32[1024,768]{1,0:T(8,128)}, f32[1024,128]{1,0:T(8,128)}, bf16[1024,768]{1,0:T(8,128)(2,1)}, f32[8,768]{1,0:T(8,128)}) custom-call(s32[1]{0:T(128)} %bitcast.me_ref, bf16[1024,768]{1,0:T(8,128)(2,1)} %get-tuple-element.41.att_ref.o_ref, bf16[1024,768]{1,0:T(8,128)(2,1)} %bitcast.57, bf16[96,3200]{1,0:T(8,128)(2,1)} %copy-done.1, ...), custom_call_target="tpu_custom_call" | custom-call | flops 1207959552 | bytes 12000000 | tf_op jit(solution)/shard_map/out_norm/pallas_call | solution.py:254
  138.6 19.8 %gate_up.1 = (bf16[1024,3072]{1,0:T(8,128)(2,1)}, bf16[1024,3072]{1,0:T(8,128)(2,1)}, bf16[1024,3072]{1,0:T(8,128)(2,1)}) custom-call(s32[1]{0:T(128)} %bitcast.me_ref, bf16[1024,768]{1,0:T(8,128)(2,1)} %get-tuple-element.42.x_ref, bf16[96,6144]{1,0:T(8,128)(2,1)} %copy-done.28, bf16[96,6144]{1,0:T(8,128)(2,1)} %copy-done.27, bf16[96,6144]{1,0:T(8,128)(2,1)} %copy-done.26, ...), custom_call_target="tpu_custom_call" | custom-call | flops 9663676416 | bytes 30000000 | tf_op jit(solution)/shard_map/gate_up/pallas_call | solution.py:306
  158.5 0.7 copy-done.18
  159.6 13.8 %down_norm.1 = (bf16[1024,768]{1,0:T(8,128)(2,1)}, f32[1024,768]{1,0:T(8,128)}, bf16[1024,768]{1,0:T(8,128)(2,1)}, f32[8,768]{1,0:T(8,128)}) custom-call(s32[1]{0:T(128)} %bitcast.me_ref, bf16[1024,3072]{1,0:T(8,128)(2,1)} %get-tuple-element.43.h_ref, f32[1024,768]{1,0:T(8,128)} %get-tuple-element.44.n1_ref, bf16[1024,768]{1,0:T(8,128)(2,1)} %bitcast.67, ...), custom_call_target="tpu_custom_call" | custom-call | flops 4831838208 | bytes 20000000 | tf_op jit(solution)/shard_map/down_norm/pallas_call | solution.py:351
  173.5 15.8 %hidden_grad.1 = (bf16[1024,3072]{1,0:T(8,128)(2,1)}, bf16[1024,3072]{1,0:T(8,128)(2,1)}) custom-call(s32[1]{0:T(128)} %bitcast.me_ref, bf16[1024,768]{1,0:T(8,128)(2,1)} %get-tuple-element.47.g_ref, bf16[1024,3072]{1,0:T(8,128)(2,1)} %get-tuple-element.48.a_ref, bf16[1024,3072]{1,0:T(8,128)(2,1)} %get-tuple-element.49.b_ref, bf16[384,768]{1,0:T(8,128)(2,1)} %rest_0_.3, ...), custom_call_target="tpu_custom_call" | custom-call | flops 4831838208 | bytes 32000000 | tf_op jit(solution)/shard_map/hidden_grad/pallas_call | solution.py:445
  189.3 24.1 %mixed_grad.1 = (f32[1024,768]{1,0:T(8,128)}, bf16[1024,768]{1,0:T(8,128)(2,1)}, bf16[1024,768]{1,0:T(8,128)(2,1)}, f32[8,768]{1,0:T(8,128)}) custom-call(s32[1]{0:T(128)} %bitcast.me_ref, bf16[1024,3072]{1,0:T(8,128)(2,1)} %get-tuple-element.50.gg_ref.g_ref, bf16[1024,3072]{1,0:T(8,128)(2,1)} %get-tuple-element.51.gu_ref.g_ref, ...), custom_call_target="tpu_custom_call" | custom-call | flops 10871635968 | bytes 36000000 | tf_op jit(solution)/shard_map/mixed_grad/pallas_call | solution.py:526
  213.4 20.6 %attend_bwd.1 = (bf16[1024,768]{1,0:T(8,128)(2,1)}, bf16[1024,768]{1,0:T(8,128)(2,1)}, bf16[1024,768]{1,0:T(8,128)(2,1)}) custom-call(bf16[1024,2304]{1,0:T(8,128)(2,1)} %qkv_rope.1.q_ref.k_ref.v_ref, bf16[1024,2304]{1,0:T(8,128)(2,1)} %qkv_rope.1.q_ref.k_ref.v_ref, bf16[1024,2304]{1,0:T(8,128)(2,1)} %qkv_rope.1.q_ref.k_ref.v_ref, ...), custom_call_target="tpu_custom_call" | custom-call | flops 12884901888 | bytes 25000000 | tf_op jit(solution)/shard_map/attend_bwd/pallas_call | solution.py:634
  234.0 8.7 %qkv_grad.1 = (bf16[4,96,2304]{2,1,0:T(8,128)(2,1)}, bf16[4,96,2304]{2,1,0:T(8,128)(2,1)}) custom-call(s32[1]{0:T(128)} %bitcast.me_ref, bf16[1024,768]{1,0:T(8,128)(2,1)} %bitcast.58, bf16[1024,768]{1,0:T(8,128)(2,1)} %get-tuple-element.57.dq_ref, bf16[1024,768]{1,0:T(8,128)(2,1)} %get-tuple-element.58.dk_ref, bf16[1024,768]{1,0:T(8,128)(2,1)} %get-tuple-element.59.dv_ref), custom_call_target="tpu_custom_call" | custom-call | flops 3623878656 | bytes 10000000 | tf_op jit(solution)/shard_map/qkv_grad/pallas_call | solution.py:664
  242.9 10.1 %down_grad.1 = (bf16[4,384,768]{2,1,0:T(8,128)(2,1)}, bf16[4,384,768]{2,1,0:T(8,128)(2,1)}) custom-call(s32[1]{0:T(128)} %bitcast.me_ref, bf16[1024,3072]{1,0:T(8,128)(2,1)} %get-tuple-element.43.h_ref, bf16[1024,768]{1,0:T(8,128)(2,1)} %get-tuple-element.47.g_ref), custom_call_target="tpu_custom_call" | custom-call | flops 4831838208 | bytes 13000000 | tf_op jit(solution)/shard_map/down_grad/pallas_call | solution.py:388
  253.4 9.5 %gate_grad.1 = (bf16[4,96,3072]{2,1,0:T(8,128)(2,1)}, bf16[4,96,3072]{2,1,0:T(8,128)(2,1)}) custom-call(s32[1]{0:T(128)} %bitcast.me_ref, bf16[1024,768]{1,0:T(8,128)(2,1)} %get-tuple-element.42.x_ref, bf16[1024,3072]{1,0:T(8,128)(2,1)} %get-tuple-element.50.gg_ref.g_ref), custom_call_target="tpu_custom_call" | custom-call | flops 4831838208 | bytes 13000000 | tf_op jit(solution)/shard_map/gate_grad/pallas_call | solution.py:473
  263.1 13.6 %up_out_grad.1 = (bf16[4,96,3968]{2,1,0:T(8,128)(2,1)}, bf16[4,96,3968]{2,1,0:T(8,128)(2,1)}) custom-call(s32[1]{0:T(128)} %bitcast.me_ref, bf16[1024,768]{1,0:T(8,128)(2,1)} %get-tuple-element.42.x_ref, bf16[1024,3072]{1,0:T(8,128)(2,1)} %get-tuple-element.51.gu_ref.g_ref, bf16[1024,768]{1,0:T(8,128)(2,1)} %get-tuple-element.41.att_ref.o_ref, ...), custom_call_target="tpu_custom_call" | custom-call | flops 6039797760 | bytes 16000000 | tf_op jit(solution)/shard_map/up_out_grad/pallas_call | solution.py:581
  277.1 2.4 add.58
  280.1 1.7 collective-permute-start.29
  281.8 10.1 %collective-permute-done.28 = bf16[96,2304]{1,0:T(8,128)(2,1)S(1)} collective-permute-done((bf16[96,2304]{1,0:T(8,128)(2,1)S(1)}, bf16[96,2304]{1,0:T(8,128)(2,1)S(1)}, u32[]{:S(2)}, u32[]{:S(2)}) %collective-permute-start.28) | collective-permute-done | bytes 442400 | tf_op jit(solution)/shard_map/ppermute | solution.py:38
  291.8 1.5 collective-permute-start.30
  293.3 10.7 %collective-permute-done.30 = bf16[96,2304]{1,0:T(8,128)(2,1)S(1)} collective-permute-done((bf16[96,2304]{1,0:T(8,128)(2,1)S(1)}, bf16[96,2304]{1,0:T(8,128)(2,1)S(1)}, u32[]{:S(2)}, u32[]{:S(2)}) %collective-permute-start.30) | collective-permute-done | bytes 442400 | tf_op jit(solution)/shard_map/ppermute | solution.py:38
  304.0 1.0 fusion.12
  305.0 2.2 add.70
  307.8 1.7 collective-permute-start.41
  309.5 1.5 collective-permute-start.42
  310.9 0.9 add.66
  312.4 1.7 collective-permute-start.37
  314.8 8.9 %collective-permute-done.40 = bf16[384,768]{1,0:T(8,128)(2,1)S(1)} collective-permute-done((bf16[384,768]{1,0:T(8,128)(2,1)S(1)}, bf16[384,768]{1,0:T(8,128)(2,1)S(1)}, u32[]{:S(2)}, u32[]{:S(2)}) %collective-permute-start.40) | collective-permute-done | bytes 589856 | tf_op jit(solution)/shard_map/ppermute | solution.py:38
  323.7 1.5 collective-permute-start.38
  325.3 10.8 %collective-permute-done.41 = bf16[384,768]{1,0:T(8,128)(2,1)S(1)} collective-permute-done((bf16[384,768]{1,0:T(8,128)(2,1)S(1)}, bf16[384,768]{1,0:T(8,128)(2,1)S(1)}, u32[]{:S(2)}, u32[]{:S(2)}) %collective-permute-start.41) | collective-permute-done | bytes 589856 | tf_op jit(solution)/shard_map/ppermute | solution.py:38
  336.1 2.3 collective-permute-start.32
  338.4 1.5 collective-permute-start.33
  339.9 9.1 %collective-permute-done.36 = bf16[96,3072]{1,0:T(8,128)(2,1)S(1)} collective-permute-done((bf16[96,3072]{1,0:T(8,128)(2,1)S(1)}, bf16[96,3072]{1,0:T(8,128)(2,1)S(1)}, u32[]{:S(2)}, u32[]{:S(2)}) %collective-permute-start.36) | collective-permute-done | bytes 589856 | tf_op jit(solution)/shard_map/ppermute | solution.py:38
  349.0 1.5 collective-permute-start.34
  350.5 1.1 fusion.6
  351.6 9.7 %collective-permute-done.37 = bf16[96,3072]{1,0:T(8,128)(2,1)S(1)} collective-permute-done((bf16[96,3072]{1,0:T(8,128)(2,1)S(1)}, bf16[96,3072]{1,0:T(8,128)(2,1)S(1)}, u32[]{:S(2)}, u32[]{:S(2)}) %collective-permute-start.37) | collective-permute-done | bytes 589856 | tf_op jit(solution)/shard_map/ppermute | solution.py:38
  361.3 1.3 collective-permute-done.38
  362.7 1.2 fusion.9
  363.8 14.2 %collective-permute-done.32 = bf16[96,3968]{1,0:T(8,128)(2,1)S(1)} collective-permute-done((bf16[96,3968]{1,0:T(8,128)(2,1)S(1)}, bf16[96,3968]{1,0:T(8,128)(2,1)S(1)}, u32[]{:S(2)}, u32[]{:S(2)}) %collective-permute-start.32) | collective-permute-done | bytes 761888 | tf_op jit(solution)/shard_map/ppermute | solution.py:38
  378.0 14.5 %collective-permute-done.34 = bf16[96,3968]{1,0:T(8,128)(2,1)S(1)} collective-permute-done((bf16[96,3968]{1,0:T(8,128)(2,1)S(1)}, bf16[96,3968]{1,0:T(8,128)(2,1)S(1)}, u32[]{:S(2)}, u32[]{:S(2)}) %collective-permute-start.34) | collective-permute-done | bytes 761888 | tf_op jit(solution)/shard_map/ppermute | solution.py:38
  392.6 1.3 fusion.2
  393.9 9.6 %input_grad.1 = bf16[1024,768]{1,0:T(8,128)(2,1)} custom-call(s32[1]{0:T(128)} %bitcast.me_ref, f32[1024,768]{1,0:T(8,128)} %get-tuple-element.54.g1_ref, bf16[1024,768]{1,0:T(8,128)(2,1)} %get-tuple-element.57.dq_ref, bf16[1024,768]{1,0:T(8,128)(2,1)} %get-tuple-element.58.dk_ref, bf16[1024,768]{1,0:T(8,128)(2,1)} %get-tuple-element.59.dv_ref, ...), custom_call_target="tpu_custom_call" | custom-call | flops 3623878656 | bytes 14000000 | tf_op jit(solution)/shard_map/input_grad/pallas_call | solution.py:696
  403.4 88.6 %all-reduce.4.cloned.1.call-done = (bf16[96,2304]{1,0:T(8,128)(2,1)}, bf16[96,3968]{1,0:T(8,128)(2,1)}, bf16[96,3072]{1,0:T(8,128)(2,1)}, bf16[384,768]{1,0:T(8,128)(2,1)}) async-done(((bf16[96,2304]{1,0:T(8,128)(2,1)}, bf16[96,3968]{1,0:T(8,128)(2,1)}, bf16[96,3072]{1,0:T(8,128)(2,1)}, bf16[384,768]{1,0:T(8,128)(2,1)}), (bf16[96,2304]{1,0:T(8,128)(2,1)}, bf16[96,3968]{1,0:T(8,128)(2,1)}, ...) | async-done | bytes 2383888 | tf_op jit(solution)/shard_map/psum | solution.py:761
  492.0 1.3 convert_element_type.113
  493.4 1.1 slice.136
  495.2 0.7 slice_reduce_fusion
  496.0 1.1 convert_element_type.120
  497.1 1.1 convert_element_type.127
  498.2 1.0 convert_element_type.106
  (141 shorter events, 12.3 us)
Async XLA Ops:
  7.2 5.3 %copy-start.23 = (bf16[96,3072]{1,0:T(8,128)(2,1)S(1)}, bf16[96,3072]{1,0:T(8,128)(2,1)}, u32[]{:S(2)}) copy-start(bf16[96,3072]{1,0:T(8,128)(2,1)} %param.16) | copy-start | bytes 1769476
  7.2 5.4 %copy-start.24 = (bf16[96,3072]{1,0:T(8,128)(2,1)S(1)}, bf16[96,3072]{1,0:T(8,128)(2,1)}, u32[]{:S(2)}) copy-start(bf16[96,3072]{1,0:T(8,128)(2,1)} %param.17) | copy-start | bytes 1769476
  7.2 484.8 %all-reduce.4.cloned.1.call-start = ((), (), s32[]{:S(2)}) async-start(), calls=%async_computation | async-start | bytes 4767744 | tf_op jit(solution)/shard_map/psum | solution.py:761
  8.2 7.9 %copy-start.16 = (bf16[384,768]{1,0:T(8,128)(2,1)S(1)}, bf16[384,768]{1,0:T(8,128)(2,1)}, u32[]{:S(2)}) copy-start(bf16[384,768]{1,0:T(8,128)(2,1)} %rest_0_.3) | copy-start | bytes 1769476
  9.4 35.4 %copy-start.1 = (bf16[96,3200]{1,0:T(8,128)(2,1)}, bf16[96,3200]{1,0:T(8,128)(2,1)S(1)}, u32[]{:S(2)}) copy-start(bf16[96,3200]{1,0:T(8,128)(2,1)S(1)} %fusion.13.rest_0_.rest_10_) | copy-start | bytes 1843204
  9.4 32.4 %collective-permute-start.1 = (bf16[96,3200]{1,0:T(8,128)(2,1)S(1)}, bf16[96,3200]{1,0:T(8,128)(2,1)S(1)}, u32[]{:S(2)}, u32[]{:S(2)}) collective-permute-start(bf16[96,3200]{1,0:T(8,128)(2,1)S(1)} %fusion.13.rest_0_.rest_10_), channel_id=1, source_target_pairs={{0,16},{4,20},{8,24},{12,28},{16,0},{20,4},{24,8},{28,12},{1,17},{... | collective-permute-start | bytes 1843208 | tf_op jit(solution)/shard_map/ppermute | solution.py:38
  12.4 27.3 %collective-permute-start.19 = (bf16[384,768]{1,0:T(8,128)(2,1)}, bf16[384,768]{1,0:T(8,128)(2,1)S(1)}, u32[]{:S(2)}, u32[]{:S(2)}) collective-permute-start(bf16[384,768]{1,0:T(8,128)(2,1)} %rest_0_.3), channel_id=1, source_target_pairs={{0,16},{4,20},{8,24},{12,28},{16,0},{20,4},{24,8},{28,12},{1,17},{... | collective-permute-start | bytes 1769480 | tf_op jit(solution)/shard_map/ppermute | solution.py:38
  12.6 80.6 %copy-start.28 = (bf16[96,6144]{1,0:T(8,128)(2,1)}, bf16[96,6144]{1,0:T(8,128)(2,1)S(1)}, u32[]{:S(2)}) copy-start(bf16[96,6144]{1,0:T(8,128)(2,1)S(1)} %constant_dynamic-update-slice_fusion.rest_0_) | copy-start | bytes 3538948
  12.6 68.3 %collective-permute-start.10 = (bf16[96,6144]{1,0:T(8,128)(2,1)S(1)}, bf16[96,6144]{1,0:T(8,128)(2,1)S(1)}, u32[]{:S(2)}, u32[]{:S(2)}) collective-permute-start(bf16[96,6144]{1,0:T(8,128)(2,1)S(1)} %constant_dynamic-update-slice_fusion.rest_0_), channel_id=1, source_target_pairs={{0,16},{4,20},{8,24},{12,28},{16,0},{20,4},{24,8},{28,12},{1,17},{... | collective-permute-start | bytes 3538952 | tf_op jit(solution)/shard_map/ppermute | solution.py:38
  14.6 30.2 %collective-permute-start = (bf16[96,3200]{1,0:T(8,128)(2,1)S(1)}, bf16[96,3200]{1,0:T(8,128)(2,1)S(1)}, u32[]{:S(2)}, u32[]{:S(2)}) collective-permute-start(bf16[96,3200]{1,0:T(8,128)(2,1)S(1)} %fusion.13.rest_0_.rest_10_), channel_id=1, source_target_pairs={{0,8},{4,12},{8,0},{12,4},{16,24},{20,28},{24,16},{28,20},{1,9},{5... | collective-permute-start | bytes 1843208 | tf_op jit(solution)/shard_map/ppermute | solution.py:38
  16.1 27.1 %collective-permute-start.18 = (bf16[384,768]{1,0:T(8,128)(2,1)S(1)}, bf16[384,768]{1,0:T(8,128)(2,1)S(1)}, u32[]{:S(2)}, u32[]{:S(2)}) collective-permute-start(bf16[384,768]{1,0:T(8,128)(2,1)S(1)} %copy-done.16), channel_id=1, source_target_pairs={{0,8},{4,12},{8,0},{12,4},{16,24},{20,28},{24,16},{28,20},{1,9},{5... | collective-permute-start | bytes 1769480 | tf_op jit(solution)/shard_map/ppermute | solution.py:38
  39.7 42.9 %copy-start.10 = (bf16[384,768]{1,0:T(8,128)(2,1)}, bf16[384,768]{1,0:T(8,128)(2,1)S(1)}, u32[]{:S(2)}) copy-start(bf16[384,768]{1,0:T(8,128)(2,1)S(1)} %collective-permute-done.19.rest_2_) | copy-start | bytes 1769476
  39.7 41.7 %collective-permute-start.9 = (bf16[96,6144]{1,0:T(8,128)(2,1)S(1)}, bf16[96,6144]{1,0:T(8,128)(2,1)S(1)}, u32[]{:S(2)}, u32[]{:S(2)}) collective-permute-start(bf16[96,6144]{1,0:T(8,128)(2,1)S(1)} %constant_dynamic-update-slice_fusion.rest_0_), channel_id=1, source_target_pairs={{0,8},{4,12},{8,0},{12,4},{16,24},{20,28},{24,16},{28,20},{1,9},{5... | collective-permute-start | bytes 3538952 | tf_op jit(solution)/shard_map/ppermute | solution.py:38
  41.8 40.8 %copy-start.2 = (bf16[96,3200]{1,0:T(8,128)(2,1)}, bf16[96,3200]{1,0:T(8,128)(2,1)S(1)}, u32[]{:S(2)}) copy-start(bf16[96,3200]{1,0:T(8,128)(2,1)S(1)} %collective-permute-done.1.rest_2_.rest_12_) | copy-start | bytes 1843204
  41.8 3.6 collective-permute-start.4
  43.2 37.7 %copy-start.12 = (bf16[384,768]{1,0:T(8,128)(2,1)}, bf16[384,768]{1,0:T(8,128)(2,1)S(1)}, u32[]{:S(2)}) copy-start(bf16[384,768]{1,0:T(8,128)(2,1)S(1)} %collective-permute-done.18.rest_1_) | copy-start | bytes 1769476
  43.2 37.0 %collective-permute-start.2 = (bf16[48,3200]{1,0:T(8,128)(2,1)S(1)}, bf16[48,3200]{1,0:T(8,128)(2,1)S(1)}, u32[]{:S(2)}, u32[]{:S(2)}) collective-permute-start(bf16[48,3200]{1,0:T(8,128)(2,1)S(1)} %slice.117), channel_id=1, source_target_pairs={{0,8},{4,12},{8,0},{12,4},{16,24},{20,28},{24,16},{28,20},{1,9},{5... | collective-permute-start | bytes 921608 | tf_op jit(solution)/shard_map/ppermute | solution.py:38
  44.8 38.7 %copy-start.3 = (bf16[96,3200]{1,0:T(8,128)(2,1)}, bf16[96,3200]{1,0:T(8,128)(2,1)S(1)}, u32[]{:S(2)}) copy-start(bf16[96,3200]{1,0:T(8,128)(2,1)S(1)} %collective-permute-done.rest_1_.rest_11_) | copy-start | bytes 1843204
  44.8 35.4 %collective-permute-start.20 = (bf16[192,768]{1,0:T(8,128)(2,1)S(1)}, bf16[192,768]{1,0:T(8,128)(2,1)S(1)}, u32[]{:S(2)}, u32[]{:S(2)}) collective-permute-start(bf16[192,768]{1,0:T(8,128)(2,1)S(1)} %slice.121), channel_id=1, source_target_pairs={{0,8},{4,12},{8,0},{12,4},{16,24},{20,28},{24,16},{28,20},{1,9},{5... | collective-permute-start | bytes 884744 | tf_op jit(solution)/shard_map/ppermute | solution.py:38
  45.4 48.9 %copy-start.5 = (bf16[96,3200]{1,0:T(8,128)(2,1)}, bf16[96,3200]{1,0:T(8,128)(2,1)S(1)}, u32[]{:S(2)}) copy-start(bf16[96,3200]{1,0:T(8,128)(2,1)S(1)} %collective-permute-done.4.rest_5_.rest_15_) | copy-start | bytes 1843204
  45.4 35.5 %collective-permute-start.3 = (bf16[48,3200]{1,0:T(8,128)(2,1)S(1)}, bf16[48,3200]{1,0:T(8,128)(2,1)}, u32[]{:S(2)}, u32[]{:S(2)}) collective-permute-start(bf16[48,3200]{1,0:T(8,128)(2,1)S(1)} %slice.118), channel_id=1, source_target_pairs={{0,16},{4,20},{8,24},{12,28},{16,0},{20,4},{24,8},{28,12},{1,17},{... | collective-permute-start | bytes 921608 | tf_op jit(solution)/shard_map/ppermute | solution.py:38
  80.2 13.1 %collective-permute-start.5 = (bf16[96,3200]{1,0:T(8,128)(2,1)S(1)}, bf16[96,3200]{1,0:T(8,128)(2,1)S(1)}, u32[]{:S(2)}, u32[]{:S(2)}) collective-permute-start(bf16[96,3200]{1,0:T(8,128)(2,1)S(1)} %collective-permute-done.rest_1_.rest_11_), channel_id=1, source_target_pairs={{0,4},{4,0},{8,12},{12,8},{16,20},{20,16},{24,28},{28,24},{1,5},{5... | collective-permute-start | bytes 1843208 | tf_op jit(solution)/shard_map/ppermute | solution.py:38
  80.2 14.1 %copy-start.14 = (bf16[48,3200]{1,0:T(8,128)(2,1)}, bf16[48,3200]{1,0:T(8,128)(2,1)S(1)}, u32[]{:S(2)}) copy-start(bf16[48,3200]{1,0:T(8,128)(2,1)S(1)} %collective-permute-done.2.rest_3_.rest_13_) | copy-start | bytes 921604
  80.2 13.6 %collective-permute-start.6 = (bf16[96,3200]{1,0:T(8,128)(2,1)S(1)}, bf16[96,3200]{1,0:T(8,128)(2,1)S(1)}, u32[]{:S(2)}, u32[]{:S(2)}) collective-permute-start(bf16[96,3200]{1,0:T(8,128)(2,1)S(1)} %collective-permute-done.1.rest_2_.rest_12_), channel_id=1, source_target_pairs={{0,4},{4,0},{8,12},{12,8},{16,20},{20,16},{24,28},{28,24},{1,5},{5... | collective-permute-start | bytes 1843208 | tf_op jit(solution)/shard_map/ppermute | solution.py:38
  80.9 11.0 %collective-permute-start.7 = (bf16[48,3200]{1,0:T(8,128)(2,1)S(1)}, bf16[48,3200]{1,0:T(8,128)(2,1)S(1)}, u32[]{:S(2)}, u32[]{:S(2)}) collective-permute-start(bf16[48,3200]{1,0:T(8,128)(2,1)S(1)} %collective-permute-done.2.rest_3_.rest_13_), channel_id=1, source_target_pairs={{0,4},{4,0},{8,12},{12,8},{16,20},{20,16},{24,28},{28,24},{1,5},{5... | collective-permute-start | bytes 921608 | tf_op jit(solution)/shard_map/ppermute | solution.py:38
  81.0 12.2 %copy-start.26 = (bf16[96,6144]{1,0:T(8,128)(2,1)}, bf16[96,6144]{1,0:T(8,128)(2,1)S(1)}, u32[]{:S(2)}) copy-start(bf16[96,6144]{1,0:T(8,128)(2,1)S(1)} %collective-permute-done.10.rest_2_) | copy-start | bytes 3538948
  81.0 9.5 %collective-permute-start.21 = (bf16[192,768]{1,0:T(8,128)(2,1)S(1)}, bf16[192,768]{1,0:T(8,128)(2,1)S(1)}, u32[]{:S(2)}, u32[]{:S(2)}) collective-permute-start(bf16[192,768]{1,0:T(8,128)(2,1)S(1)} %slice.122), channel_id=1, source_target_pairs={{0,16},{4,20},{8,24},{12,28},{16,0},{20,4},{24,8},{28,12},{1,17},{... | collective-permute-start | bytes 884744 | tf_op jit(solution)/shard_map/ppermute | solution.py:38
  81.4 11.8 %copy-start.27 = (bf16[96,6144]{1,0:T(8,128)(2,1)}, bf16[96,6144]{1,0:T(8,128)(2,1)S(1)}, u32[]{:S(2)}) copy-start(bf16[96,6144]{1,0:T(8,128)(2,1)S(1)} %collective-permute-done.9.rest_1_) | copy-start | bytes 3538948
  81.4 11.8 %collective-permute-start.8 = (bf16[48,3200]{1,0:T(8,128)(2,1)}, bf16[48,3200]{1,0:T(8,128)(2,1)}, u32[]{:S(2)}, u32[]{:S(2)}) collective-permute-start(bf16[48,3200]{1,0:T(8,128)(2,1)} %collective-permute-done.3.rest_4_.rest_14_), channel_id=1, source_target_pairs={{0,4},{4,0},{8,12},{12,8},{16,20},{20,16},{24,28},{28,24},{1,5},{5... | collective-permute-start | bytes 921608 | tf_op jit(solution)/shard_map/ppermute | solution.py:38
  82.6 13.4 %copy-start.31 = (s32[2,512]{1,0:T(2,128)S(1)}, s32[2,512]{1,0:T(2,128)}, u32[]{:S(2)}) copy-start(s32[2,512]{1,0:T(2,128)} %param.13) | copy-start | bytes 12292
  90.5 21.5 %collective-permute-start.11 = (bf16[48,6144]{1,0:T(8,128)(2,1)}, bf16[48,6144]{1,0:T(8,128)(2,1)}, u32[]{:S(2)}, u32[]{:S(2)}) collective-permute-start(bf16[48,6144]{1,0:T(8,128)(2,1)} %slice.119), channel_id=1, source_target_pairs={{0,8},{4,12},{8,0},{12,4},{16,24},{20,28},{24,16},{28,20},{1,9},{5... | collective-permute-start | bytes 1769480 | tf_op jit(solution)/shard_map/ppermute | solution.py:38
  92.7 19.7 %collective-permute-start.12 = (bf16[48,6144]{1,0:T(8,128)(2,1)}, bf16[48,6144]{1,0:T(8,128)(2,1)}, u32[]{:S(2)}, u32[]{:S(2)}) collective-permute-start(bf16[48,6144]{1,0:T(8,128)(2,1)} %slice.120), channel_id=1, source_target_pairs={{0,16},{4,20},{8,24},{12,28},{16,0},{20,4},{24,8},{28,12},{1,17},{... | collective-permute-start | bytes 1769480 | tf_op jit(solution)/shard_map/ppermute | solution.py:38
  93.3 43.8 %collective-permute-start.13 = (bf16[96,6144]{1,0:T(8,128)(2,1)}, bf16[96,6144]{1,0:T(8,128)(2,1)}, u32[]{:S(2)}, u32[]{:S(2)}) collective-permute-start(bf16[96,6144]{1,0:T(8,128)(2,1)} %copy-done.28), channel_id=1, source_target_pairs={{0,4},{4,0},{8,12},{12,8},{16,20},{20,16},{24,28},{28,24},{1,5},{5... | collective-permute-start | bytes 3538952 | tf_op jit(solution)/shard_map/ppermute | solution.py:38
  93.4 4.3 copy-start.6
  93.4 44.8 %collective-permute-start.14 = (bf16[96,6144]{1,0:T(8,128)(2,1)}, bf16[96,6144]{1,0:T(8,128)(2,1)}, u32[]{:S(2)}, u32[]{:S(2)}) collective-permute-start(bf16[96,6144]{1,0:T(8,128)(2,1)} %copy-done.27), channel_id=1, source_target_pairs={{0,4},{4,0},{8,12},{12,8},{16,20},{20,16},{24,28},{28,24},{1,5},{5... | collective-permute-start | bytes 3538952 | tf_op jit(solution)/shard_map/ppermute | solution.py:38
  93.8 3.8 copy-start.7
  93.9 44.4 %collective-permute-start.15 = (bf16[96,6144]{1,0:T(8,128)(2,1)}, bf16[96,6144]{1,0:T(8,128)(2,1)}, u32[]{:S(2)}, u32[]{:S(2)}) collective-permute-start(bf16[96,6144]{1,0:T(8,128)(2,1)} %copy-done.26), channel_id=1, source_target_pairs={{0,4},{4,0},{8,12},{12,8},{16,20},{20,16},{24,28},{28,24},{1,5},{5... | collective-permute-start | bytes 3538952 | tf_op jit(solution)/shard_map/ppermute | solution.py:38
  112.0 25.6 %collective-permute-start.16 = (bf16[48,6144]{1,0:T(8,128)(2,1)}, bf16[48,6144]{1,0:T(8,128)(2,1)}, u32[]{:S(2)}, u32[]{:S(2)}) collective-permute-start(bf16[48,6144]{1,0:T(8,128)(2,1)} %collective-permute-done.11.rest_3_), channel_id=1, source_target_pairs={{0,4},{4,0},{8,12},{12,8},{16,20},{20,16},{24,28},{28,24},{1,5},{5... | collective-permute-start | bytes 1769480 | tf_op jit(solution)/shard_map/ppermute | solution.py:38
  112.4 25.3 %collective-permute-start.17 = (bf16[48,6144]{1,0:T(8,128)(2,1)}, bf16[48,6144]{1,0:T(8,128)(2,1)}, u32[]{:S(2)}, u32[]{:S(2)}) collective-permute-start(bf16[48,6144]{1,0:T(8,128)(2,1)} %collective-permute-done.12.rest_4_), channel_id=1, source_target_pairs={{0,4},{4,0},{8,12},{12,8},{16,20},{20,16},{24,28},{28,24},{1,5},{5... | collective-permute-start | bytes 1769480 | tf_op jit(solution)/shard_map/ppermute | solution.py:38
  129.9 7.2 %copy-start.17 = (bf16[384,768]{1,0:T(8,128)(2,1)S(1)}, bf16[384,768]{1,0:T(8,128)(2,1)}, u32[]{:S(2)}) copy-start(bf16[384,768]{1,0:T(8,128)(2,1)} %rest_0_.3) | copy-start | bytes 1769476
  129.9 7.7 %copy-start.13 = (bf16[384,768]{1,0:T(8,128)(2,1)S(1)}, bf16[384,768]{1,0:T(8,128)(2,1)}, u32[]{:S(2)}) copy-start(bf16[384,768]{1,0:T(8,128)(2,1)} %copy-done.12) | copy-start | bytes 1769476
  129.9 7.8 %copy-start.11 = (bf16[384,768]{1,0:T(8,128)(2,1)S(1)}, bf16[384,768]{1,0:T(8,128)(2,1)}, u32[]{:S(2)}) copy-start(bf16[384,768]{1,0:T(8,128)(2,1)} %copy-done.10) | copy-start | bytes 1769476
  137.1 21.3 %collective-permute-start.22 = (bf16[384,768]{1,0:T(8,128)(2,1)S(1)}, bf16[384,768]{1,0:T(8,128)(2,1)S(1)}, u32[]{:S(2)}, u32[]{:S(2)}) collective-permute-start(bf16[384,768]{1,0:T(8,128)(2,1)S(1)} %copy-done.17), channel_id=1, source_target_pairs={{0,4},{4,0},{8,12},{12,8},{16,20},{20,16},{24,28},{28,24},{1,5},{5... | collective-permute-start | bytes 1769480 | tf_op jit(solution)/shard_map/ppermute | solution.py:38
  137.6 20.9 %collective-permute-start.23 = (bf16[384,768]{1,0:T(8,128)(2,1)S(1)}, bf16[384,768]{1,0:T(8,128)(2,1)S(1)}, u32[]{:S(2)}, u32[]{:S(2)}) collective-permute-start(bf16[384,768]{1,0:T(8,128)(2,1)S(1)} %copy-done.13), channel_id=1, source_target_pairs={{0,4},{4,0},{8,12},{12,8},{16,20},{20,16},{24,28},{28,24},{1,5},{5... | collective-permute-start | bytes 1769480 | tf_op jit(solution)/shard_map/ppermute | solution.py:38
  137.7 20.8 %collective-permute-start.24 = (bf16[384,768]{1,0:T(8,128)(2,1)S(1)}, bf16[384,768]{1,0:T(8,128)(2,1)S(1)}, u32[]{:S(2)}, u32[]{:S(2)}) collective-permute-start(bf16[384,768]{1,0:T(8,128)(2,1)S(1)} %copy-done.11), channel_id=1, source_target_pairs={{0,4},{4,0},{8,12},{12,8},{16,20},{20,16},{24,28},{28,24},{1,5},{5... | collective-permute-start | bytes 1769480 | tf_op jit(solution)/shard_map/ppermute | solution.py:38
  138.1 20.3 %collective-permute-start.25 = (bf16[192,768]{1,0:T(8,128)(2,1)}, bf16[192,768]{1,0:T(8,128)(2,1)}, u32[]{:S(2)}, u32[]{:S(2)}) collective-permute-start(bf16[192,768]{1,0:T(8,128)(2,1)} %copy-done.29), channel_id=1, source_target_pairs={{0,4},{4,0},{8,12},{12,8},{16,20},{20,16},{24,28},{28,24},{1,5},{5... | collective-permute-start | bytes 884744 | tf_op jit(solution)/shard_map/ppermute | solution.py:38
  138.2 20.2 %collective-permute-start.26 = (bf16[192,768]{1,0:T(8,128)(2,1)}, bf16[192,768]{1,0:T(8,128)(2,1)}, u32[]{:S(2)}, u32[]{:S(2)}) collective-permute-start(bf16[192,768]{1,0:T(8,128)(2,1)} %copy-done.30), channel_id=1, source_target_pairs={{0,4},{4,0},{8,12},{12,8},{16,20},{20,16},{24,28},{28,24},{1,5},{5... | collective-permute-start | bytes 884744 | tf_op jit(solution)/shard_map/ppermute | solution.py:38
  242.8 34.4 %collective-permute-start.27 = (bf16[4,96,2304]{2,1,0:T(8,128)(2,1)}, bf16[4,96,2304]{2,1,0:T(8,128)(2,1)}, u32[]{:S(2)}, u32[]{:S(2)}) collective-permute-start(bf16[4,96,2304]{2,1,0:T(8,128)(2,1)} %get-tuple-element.61), channel_id=1, source_target_pairs={{0,4},{4,0},{8,12},{12,8},{16,20},{20,16},{24,28},{28,24},{1,5},{5... | collective-permute-start | bytes 5308424 | tf_op jit(solution)/shard_map/ppermute | solution.py:38
  253.0 52.0 %collective-permute-start.39 = (bf16[4,384,768]{2,1,0:T(8,128)(2,1)}, bf16[4,384,768]{2,1,0:T(8,128)(2,1)}, u32[]{:S(2)}, u32[]{:S(2)}) collective-permute-start(bf16[4,384,768]{2,1,0:T(8,128)(2,1)} %get-tuple-element.70), channel_id=1, source_target_pairs={{0,4},{4,0},{8,12},{12,8},{16,20},{20,16},{24,28},{28,24},{1,5},{5... | collective-permute-start | bytes 7077896 | tf_op jit(solution)/shard_map/ppermute | solution.py:38
  263.0 47.9 %collective-permute-start.35 = (bf16[4,96,3072]{2,1,0:T(8,128)(2,1)}, bf16[4,96,3072]{2,1,0:T(8,128)(2,1)S(1)}, u32[]{:S(2)}, u32[]{:S(2)}) collective-permute-start(bf16[4,96,3072]{2,1,0:T(8,128)(2,1)} %get-tuple-element.68), channel_id=1, source_target_pairs={{0,4},{4,0},{8,12},{12,8},{16,20},{20,16},{24,28},{28,24},{1,5},{5... | collective-permute-start | bytes 7077896 | tf_op jit(solution)/shard_map/ppermute | solution.py:38
  276.7 35.7 %collective-permute-start.31 = (bf16[4,96,3968]{2,1,0:T(8,128)(2,1)}, bf16[4,96,3968]{2,1,0:T(8,128)(2,1)S(1)}, u32[]{:S(2)}, u32[]{:S(2)}) collective-permute-start(bf16[4,96,3968]{2,1,0:T(8,128)(2,1)} %get-tuple-element.66), channel_id=1, source_target_pairs={{0,4},{4,0},{8,12},{12,8},{16,20},{20,16},{24,28},{28,24},{1,5},{5... | collective-permute-start | bytes 9142280 | tf_op jit(solution)/shard_map/ppermute | solution.py:38
  279.5 25.5 %copy-start.9 = (bf16[4,384,768]{2,1,0:T(8,128)(2,1)S(1)}, bf16[4,384,768]{2,1,0:T(8,128)(2,1)}, u32[]{:S(2)}) copy-start(bf16[4,384,768]{2,1,0:T(8,128)(2,1)} %get-tuple-element.69) | copy-start | bytes 7077892
  279.7 12.2 %collective-permute-start.28 = (bf16[96,2304]{1,0:T(8,128)(2,1)S(1)}, bf16[96,2304]{1,0:T(8,128)(2,1)S(1)}, u32[]{:S(2)}, u32[]{:S(2)}) collective-permute-start(bf16[96,2304]{1,0:T(8,128)(2,1)S(1)} %get-tuple-element.88), channel_id=1, source_target_pairs={{0,8},{4,12},{8,0},{12,4},{16,24},{20,28},{24,16},{28,20},{1,9},{5... | collective-permute-start | bytes 1327112 | tf_op jit(solution)/shard_map/ppermute | solution.py:38
  280.1 13.2 %collective-permute-start.29 = (bf16[96,2304]{1,0:T(8,128)(2,1)S(1)}, bf16[96,2304]{1,0:T(8,128)(2,1)S(1)}, u32[]{:S(2)}, u32[]{:S(2)}) collective-permute-start(bf16[96,2304]{1,0:T(8,128)(2,1)S(1)} %get-tuple-element.90), channel_id=1, source_target_pairs={{0,16},{4,20},{8,24},{12,28},{16,0},{20,4},{24,8},{28,12},{1,17},{... | collective-permute-start | bytes 1327112 | tf_op jit(solution)/shard_map/ppermute | solution.py:38
  291.8 12.2 %collective-permute-start.30 = (bf16[96,2304]{1,0:T(8,128)(2,1)S(1)}, bf16[96,2304]{1,0:T(8,128)(2,1)S(1)}, u32[]{:S(2)}, u32[]{:S(2)}) collective-permute-start(bf16[96,2304]{1,0:T(8,128)(2,1)S(1)} %get-tuple-element.89), channel_id=1, source_target_pairs={{0,24},{4,28},{8,16},{12,20},{16,8},{20,12},{24,0},{28,4},{1,25},{... | collective-permute-start | bytes 1327112 | tf_op jit(solution)/shard_map/ppermute | solution.py:38
  307.4 16.3 %collective-permute-start.40 = (bf16[384,768]{1,0:T(8,128)(2,1)S(1)}, bf16[384,768]{1,0:T(8,128)(2,1)S(1)}, u32[]{:S(2)}, u32[]{:S(2)}) collective-permute-start(bf16[384,768]{1,0:T(8,128)(2,1)S(1)} %get-tuple-element.82), channel_id=1, source_target_pairs={{0,8},{4,12},{8,0},{12,4},{16,24},{20,28},{24,16},{28,20},{1,9},{5... | collective-permute-start | bytes 1769480 | tf_op jit(solution)/shard_map/ppermute | solution.py:38
  307.8 28.3 %collective-permute-start.41 = (bf16[384,768]{1,0:T(8,128)(2,1)S(1)}, bf16[384,768]{1,0:T(8,128)(2,1)S(1)}, u32[]{:S(2)}, u32[]{:S(2)}) collective-permute-start(bf16[384,768]{1,0:T(8,128)(2,1)S(1)} %get-tuple-element.84), channel_id=1, source_target_pairs={{0,16},{4,20},{8,24},{12,28},{16,0},{20,4},{24,8},{28,12},{1,17},{... | collective-permute-start | bytes 1769480 | tf_op jit(solution)/shard_map/ppermute | solution.py:38
  309.5 28.9 %collective-permute-start.42 = (bf16[384,768]{1,0:T(8,128)(2,1)S(1)}, bf16[384,768]{1,0:T(8,128)(2,1)S(1)}, u32[]{:S(2)}, u32[]{:S(2)}) collective-permute-start(bf16[384,768]{1,0:T(8,128)(2,1)S(1)} %get-tuple-element.83), channel_id=1, source_target_pairs={{0,24},{4,28},{8,16},{12,20},{16,8},{20,12},{24,0},{28,4},{1,25},{... | collective-permute-start | bytes 1769480 | tf_op jit(solution)/shard_map/ppermute | solution.py:38
  311.9 37.1 %collective-permute-start.36 = (bf16[96,3072]{1,0:T(8,128)(2,1)S(1)}, bf16[96,3072]{1,0:T(8,128)(2,1)S(1)}, u32[]{:S(2)}, u32[]{:S(2)}) collective-permute-start(bf16[96,3072]{1,0:T(8,128)(2,1)S(1)} %get-tuple-element.85), channel_id=1, source_target_pairs={{0,8},{4,12},{8,0},{12,4},{16,24},{20,28},{24,16},{28,20},{1,9},{5... | collective-permute-start | bytes 1769480 | tf_op jit(solution)/shard_map/ppermute | solution.py:38
  312.4 48.9 %collective-permute-start.37 = (bf16[96,3072]{1,0:T(8,128)(2,1)S(1)}, bf16[96,3072]{1,0:T(8,128)(2,1)S(1)}, u32[]{:S(2)}, u32[]{:S(2)}) collective-permute-start(bf16[96,3072]{1,0:T(8,128)(2,1)S(1)} %get-tuple-element.87), channel_id=1, source_target_pairs={{0,16},{4,20},{8,24},{12,28},{16,0},{20,4},{24,8},{28,12},{1,17},{... | collective-permute-start | bytes 1769480 | tf_op jit(solution)/shard_map/ppermute | solution.py:38
  323.7 39.0 %collective-permute-start.38 = (bf16[96,3072]{1,0:T(8,128)(2,1)S(1)}, bf16[96,3072]{1,0:T(8,128)(2,1)S(1)}, u32[]{:S(2)}, u32[]{:S(2)}) collective-permute-start(bf16[96,3072]{1,0:T(8,128)(2,1)S(1)} %get-tuple-element.86), channel_id=1, source_target_pairs={{0,24},{4,28},{8,16},{12,20},{16,8},{20,12},{24,0},{28,4},{1,25},{... | collective-permute-start | bytes 1769480 | tf_op jit(solution)/shard_map/ppermute | solution.py:38
  336.1 41.9 %collective-permute-start.32 = (bf16[96,3968]{1,0:T(8,128)(2,1)S(1)}, bf16[96,3968]{1,0:T(8,128)(2,1)S(1)}, u32[]{:S(2)}, u32[]{:S(2)}) collective-permute-start(bf16[96,3968]{1,0:T(8,128)(2,1)S(1)} %get-tuple-element.79), channel_id=1, source_target_pairs={{0,8},{4,12},{8,0},{12,4},{16,24},{20,28},{24,16},{28,20},{1,9},{5... | collective-permute-start | bytes 2285576 | tf_op jit(solution)/shard_map/ppermute | solution.py:38
  338.4 39.7 %collective-permute-start.33 = (bf16[96,3968]{1,0:T(8,128)(2,1)S(1)}, bf16[96,3968]{1,0:T(8,128)(2,1)S(1)}, u32[]{:S(2)}, u32[]{:S(2)}) collective-permute-start(bf16[96,3968]{1,0:T(8,128)(2,1)S(1)} %get-tuple-element.81), channel_id=1, source_target_pairs={{0,16},{4,20},{8,24},{12,28},{16,0},{20,4},{24,8},{28,12},{1,17},{... | collective-permute-start | bytes 2285576 | tf_op jit(solution)/shard_map/ppermute | solution.py:38
  349.0 43.5 %collective-permute-start.34 = (bf16[96,3968]{1,0:T(8,128)(2,1)S(1)}, bf16[96,3968]{1,0:T(8,128)(2,1)S(1)}, u32[]{:S(2)}, u32[]{:S(2)}) collective-permute-start(bf16[96,3968]{1,0:T(8,128)(2,1)S(1)} %get-tuple-element.80), channel_id=1, source_target_pairs={{0,24},{4,28},{8,16},{12,20},{16,8},{20,12},{24,0},{28,4},{1,25},{... | collective-permute-start | bytes 2285576 | tf_op jit(solution)/shard_map/ppermute | solution.py:38
  (12 other events, 21.9 us)
Sparse Core Ops, SparseCore 0:
  394.0 98.0 all-reduce.3
